TPU v7x, 32 devices: a whole 2x2x4 slice. The times are simulated.
32 devices in a mesh: ctx: 8 (over z, y), exp: 4 (over x, core).
Axes of the slice: x: 2, y: 2, z: 4, core: 2. Of those that a mesh axis runs over, the one named last changes fastest.
Arguments:
- frames: bfloat16 [4, 768, 2048], P('exp', 'ctx'), may hold values from -6 to 6
- queries: bfloat16 [4, 768, 2048], P('exp', 'ctx'), may hold values from -8 to 8
- keys: bfloat16 [4, 768, 2048], P('exp', 'ctx'), may hold values from -8 to 8
- values: bfloat16 [4, 768, 2048], P('exp', 'ctx'), may hold values from -6 to 6
- expert_ids: int32 [4, 768, 2], P('exp', 'ctx'), may hold values from 0 to 7, all different within a row; in each aligned block of 96 rows (0 to 95, 96 to 191, ..., all dimensions but the last counted through in order) at most 48 rows name the same one
- gate_weights: float32 [4, 768, 2], P('exp', 'ctx'), may hold values from 0.2 to 1
- w_in: bfloat16 [8, 2048, 8192], P('exp', None, 'ctx'), may hold values from -0.125 to 0.125
- w_out: bfloat16 [8, 8192, 2048], P('exp', 'ctx'), may hold values from -0.0625 to 0.0625
Outputs:
- layer_out: bfloat16 [4, 768, 2048], P('exp', 'ctx')
Inputs may be any that keep to these rules, and one draw needn't show every extreme that they name: `expert_ids`: each row names two different experts; within the rows of one device no expert is named by more than 48 rows, a bound that some block reaches.
All inputs are finite; a program needn't handle non-finite values.
Results may differ from a plain program's by a relative error of at most 0.013.
Values may be sent and summed in bfloat16 or wider, within the bound.
No kernel may reach another device: no remote copies, remote signals or barrier semaphores. Data moves between devices by JAX's collectives and lax.ppermute only.
A program may use at most 192 MiB of HBM per device.

v0:
```python
import math

import jax
import jax.numpy as jnp
from jax import lax
from jax.sharding import PartitionSpec as P

HEADS = 16
HD = 128


EPSILON = 1e-05


def gelu_tanh(values_in):
    return jax.nn.gelu(values_in, approximate=True)


def expert_partial(gathered, live_flags, first_w, second_w):
    total_rows = gathered.shape[0]
    out_width = second_w.shape[1]
    padded_rows = -(-total_rows // 128) * 128
    position = jnp.cumsum(live_flags) - 1
    live_count = jnp.sum(live_flags)
    target = jnp.where(live_flags > 0, position, padded_rows)
    order_idx = (
        jnp.zeros((padded_rows,), jnp.int32)
        .at[target]
        .set(jnp.arange(total_rows, dtype=jnp.int32), mode="drop")
    )
    block_count = (live_count + 127) // 128

    def one_block(block_num, packed):
        picked = lax.dynamic_slice_in_dim(order_idx, block_num * 128, 128)
        inputs = jnp.take(gathered, picked, axis=0)
        inner_act = gelu_tanh(jnp.dot(inputs, first_w, preferred_element_type=jnp.float32)).astype(
            jnp.bfloat16
        )
        output = jnp.dot(inner_act, second_w, preferred_element_type=jnp.float32).astype(
            jnp.bfloat16
        )
        return lax.dynamic_update_slice_in_dim(packed, output, block_num * 128, 0)

    packed = lax.fori_loop(
        0, block_count, one_block, jnp.zeros((padded_rows, out_width), jnp.bfloat16)
    )
    back_idx = jnp.where(live_flags > 0, position, 0).astype(jnp.int32)
    unpacked = jnp.take(packed, back_idx, axis=0)
    return jnp.where((live_flags > 0)[:, None], unpacked, jnp.zeros_like(unpacked))


def on_device(frames, queries, keys, values, expert_ids, gate_weights, w_in, w_out):
    tok_count = frames.shape[1]
    model_width = frames.shape[2]
    factor = 1.0 / math.sqrt(HD)
    query_heads = queries[0].reshape(tok_count, HEADS, HD)
    top_prev = jnp.full((HEADS, tok_count), -1e30, jnp.float32)
    key_piece = lax.all_gather(keys, "ctx", axis=1, tiled=True)
    value_piece = lax.all_gather(values, "ctx", axis=1, tiled=True)
    piece_len = key_piece.shape[1]
    key_heads = key_piece[0].reshape(piece_len, HEADS, HD)
    value_heads = value_piece[0].reshape(piece_len, HEADS, HD)
    scores = (
        jnp.einsum("qhd,khd->hqk", query_heads, key_heads, preferred_element_type=jnp.float32)
        * factor
    )
    top_next = jnp.maximum(top_prev, jnp.max(scores, axis=-1))
    weights_raw = jnp.exp(scores - top_next[..., None])
    total_next = jnp.sum(weights_raw, axis=-1)
    accum = jnp.einsum(
        "hqk,khd->hqd",
        weights_raw.astype(jnp.bfloat16),
        value_heads,
        preferred_element_type=jnp.float32,
    )
    top_final, total_final, accum = (top_next, total_next, accum)
    attended = jnp.transpose(accum / total_final[..., None], (1, 0, 2)).reshape(
        tok_count, HEADS * HD
    )
    hidden_state = (frames[0].astype(jnp.float32) + attended).astype(jnp.bfloat16)
    hidden_f = hidden_state.astype(jnp.float32)
    normed = (
        hidden_f * lax.rsqrt(jnp.mean(hidden_f * hidden_f, axis=-1, keepdims=True) + EPSILON)
    ).astype(jnp.bfloat16)
    slot_ids = expert_ids[0].reshape(-1)
    slot_count = slot_ids.shape[0]
    exp_local = w_in.shape[0]
    num_experts = exp_local * lax.axis_size("exp")
    capacity = 2 * (slot_count // num_experts)
    onehot = (slot_ids[:, None] == jnp.arange(num_experts, dtype=jnp.int32)[None, :]).astype(
        jnp.int32
    )
    slot_rank = jnp.sum((jnp.cumsum(onehot, axis=0) - onehot) * onehot, axis=1)
    sending = jnp.ones((slot_count,), bool)
    target = slot_ids * capacity + slot_rank
    send_matrix = (
        (jnp.arange(num_experts * capacity, dtype=jnp.int32)[:, None] == target[None, :])
        & sending[None, :]
    ).astype(jnp.int32)
    token_matrix = send_matrix.reshape(num_experts * capacity, tok_count, 2).sum(-1)
    outgoing = jnp.dot(
        token_matrix.astype(jnp.bfloat16), normed, preferred_element_type=jnp.float32
    ).astype(jnp.bfloat16)
    outgoing = outgoing.reshape(num_experts, capacity, model_width)
    occupied = jnp.sum(send_matrix, axis=1).reshape(num_experts, capacity)
    arrived, arrived_flags = (
        lax.all_to_all(outgoing, "exp", split_axis=0, concat_axis=1, tiled=True),
        lax.all_to_all(occupied, "exp", split_axis=0, concat_axis=1, tiled=True),
    )
    gathered, gathered_flags = (
        lax.all_gather(arrived, "ctx", axis=1, tiled=True),
        lax.all_gather(arrived_flags, "ctx", axis=1, tiled=True),
    )
    summed_list = []
    for local_num in range(exp_local):
        partial_value = expert_partial(
            gathered[local_num], gathered_flags[local_num], w_in[local_num], w_out[local_num]
        )
        summed_list.append(
            lax.psum_scatter(partial_value, "ctx", scatter_dimension=0, tiled=True)
            .astype(jnp.float32)
            .astype(jnp.bfloat16)
        )
    summed = jnp.stack(summed_list)
    returned = lax.all_to_all(summed, "exp", split_axis=1, concat_axis=0, tiled=True)
    slot_out = jnp.dot(
        send_matrix.T.astype(jnp.bfloat16),
        returned.reshape(num_experts * capacity, model_width),
        preferred_element_type=jnp.float32,
    )
    tok_out = slot_out.reshape(tok_count, 2, model_width)
    gates = gate_weights[0]
    layer_out = hidden_f + gates[:, 0:1] * tok_out[:, 0] + gates[:, 1:2] * tok_out[:, 1]
    return layer_out.astype(jnp.bfloat16)[None]


def solution(mesh):
    in_specs = (
        P("exp", "ctx", None),
        P("exp", "ctx", None),
        P("exp", "ctx", None),
        P("exp", "ctx", None),
        P("exp", "ctx", None),
        P("exp", "ctx", None),
        P("exp", None, "ctx"),
        P("exp", "ctx", None),
    )
    out_specs = P("exp", "ctx", None)
    return jax.shard_map(
        on_device, mesh=mesh, in_specs=in_specs, out_specs=out_specs, check_vma=False
    )
```

profile of v0, /device:TPU:0, one launch (start us, length us, event | category | flops | bytes accessed | tf_op | source)
XLA Modules:
  0.0 784.0 jit_solution(5211220962148055830)
XLA Ops:
  14.1 58.6 %all-gather.5.cloned.1.call-done = bf16[1,768,2048]{2,1,0:T(8,128)(2,1)} async-done(((bf16[1,96,2048]{2,1,0:T(8,128)(2,1)}), bf16[1,768,2048]{2,1,0:T(8,128)(2,1)}) %all-gather.5.cloned.1.call-update) | async-done | bytes 3145744 | tf_op jit(solution)/shard_map/all_gather | solution.py:58
  80.1 54.0 %all-gather.7.cloned.1.call-done = bf16[1,768,2048]{2,1,0:T(8,128)(2,1)} async-done(((bf16[1,96,2048]{2,1,0:T(8,128)(2,1)}), bf16[1,768,2048]{2,1,0:T(8,128)(2,1)}) %all-gather.7.cloned.1.call-update) | async-done | bytes 3145744 | tf_op jit(solution)/shard_map/all_gather | solution.py:59
  138.8 5.5 multiply_reduce_fusion.1
  144.9 22.6 %all_to_all.52 = bf16[8,48,2048]{2,1,0:T(8,128)(2,1)S(1)} all-to-all(bf16[8,48,2048]{2,1,0:T(8,128)(2,1)S(1)} %bitcast.146), channel_id=1, replica_groups=mesh['ctx'=8,'exp'=4] {'exp'}, dimensions={0} | all-to-all | bytes 3145728 | tf_op jit(solution)/shard_map/all_to_all | solution.py:107
  173.0 7.3 slice_bitcast_fusion.5
  180.2 6.1 slice_bitcast_fusion.4
  186.4 26.8 %all-gather = s32[8,192,2]{1,2,0:T(2,128)S(1)} all-gather(s32[1,192,2]{1,2,0:T(2,128)S(1)} %bitcast.162), channel_id=1, replica_groups=mesh['ctx'=8,'exp'=4] {'ctx'}, dimensions={0}, use_global_device_ids=true | all-gather | bytes 13824 | tf_op jit(solution)/shard_map/all_gather | solution.py:112
  215.8 6.2 scatter_custom_fusion
  222.1 121.3 %all-gather.9.cloned.1.call-done = bf16[2,1536,2048]{2,1,0:T(8,128)(2,1)} async-done(((bf16[2,192,2048]{2,1,0:T(8,128)(2,1)}), bf16[2,1536,2048]{2,1,0:T(8,128)(2,1)}) %all-gather.9.cloned.1.call-update) | async-done | bytes 12582928 | tf_op jit(solution)/shard_map/all_gather | solution.py:111
  343.4 10.7 %slice_bitcast_fusion.1 = (bf16[1536,2048]{1,0:T(8,128)(2,1)}, bf16[1536,2048]{1,0:T(8,128)(2,1)}) fusion(bf16[2,1536,2048]{2,1,0:T(8,128)(2,1)} %all-gather.9.cloned.1.call-done), kind=kLoop, calls=%fused_computation.61 | loop fusion | bytes 25165824 | tf_op jit(solution)/shard_map/squeeze | solution.py:117
  357.5 32.7 %while.20 = (s32[]{:T(128)}, bf16[1536,2048]{1,0:T(8,128)(2,1)}, s32[]{:T(128)}, s32[1536]{0:T(1024)S(1)}, bf16[1536,2048]{1,0:T(8,128)(2,1)}, /*index=5*/bf16[2...) while((s32[]{:T(128)}, bf16[1536,2048]{1,0:T(8,128)(2,1)}, ...), condition=%wide.region_13.15_spmd, body=%wide.region_12.14_spmd.sunk | while | flops 1075447552 | bytes 10492323 | solution.py:44
  357.6 5.0 gather_fusion
  362.6 5.8 fusion.118
  368.5 5.0 gather_fusion
  373.5 5.8 fusion.118
  384.4 5.8 fusion.118
  390.2 16.3 %gather_fusion.2 = bf16[1536,2048]{1,0:T(8,128)(2,1)} fusion(bf16[1536,2048]{1,0:T(8,128)(2,1)} %get-tuple-element.83, s32[2048]{0:T(1024)S(1)} %pad_clamp_fusion.3), kind=kCustom, calls=%fused_computation.1.clone | custom fusion | bytes 12589056 | tf_op jit(solution)/shard_map/jit(_take)/gather | solution.py:48
  406.5 7.1 select_select_fusion.1
  414.2 6.2 scatter_custom_fusion.1
  424.0 54.5 %while.21 = (s32[]{:T(128)}, bf16[1536,2048]{1,0:T(8,128)(2,1)}, s32[]{:T(128)}, s32[1536]{0:T(1024)S(1)}, bf16[1536,2048]{1,0:T(8,128)(2,1)}, /*index=5*/bf16[2...) while((s32[]{:T(128)}, bf16[1536,2048]{1,0:T(8,128)(2,1)}, ...), condition=%wide.region_20.23_spmd, body=%wide.region_19.22_spmd.sunk | while | flops 1075447552 | bytes 10492323 | solution.py:44
  429.1 5.8 fusion.122
  435.0 5.0 gather_fusion.1
  440.0 5.8 fusion.122
  445.9 5.0 gather_fusion.1
  450.9 5.8 fusion.122
  461.8 5.8 fusion.122
  472.7 5.8 fusion.122
  478.5 16.3 %gather_fusion.3 = bf16[1536,2048]{1,0:T(8,128)(2,1)} fusion(bf16[1536,2048]{1,0:T(8,128)(2,1)} %get-tuple-element.84, s32[2048]{0:T(1024)S(1)} %pad_clamp_fusion.2), kind=kCustom, calls=%fused_computation.3.clone | custom fusion | bytes 12589056 | tf_op jit(solution)/shard_map/jit(_take)/gather | solution.py:48
  494.8 7.0 select_select_fusion
  501.8 124.9 %reduce-scatter.3.cloned.1.call-done = bf16[192,2048]{1,0:T(8,128)(2,1)} async-done(((bf16[1536,2048]{1,0:T(8,128)(2,1)}), bf16[192,2048]{1,0:T(8,128)(2,1)}) %reduce-scatter.3.cloned.1.call-update) | async-done | bytes 786448 | tf_op jit(solution)/shard_map/reduce_scatter | solution.py:120
  626.7 120.6 %reduce-scatter.5.cloned.1.call-done = bf16[192,2048]{1,0:T(8,128)(2,1)} async-done(((bf16[1536,2048]{1,0:T(8,128)(2,1)}), bf16[192,2048]{1,0:T(8,128)(2,1)}) %reduce-scatter.5.cloned.1.call-update) | async-done | bytes 786448 | tf_op jit(solution)/shard_map/reduce_scatter | solution.py:120
  755.8 19.4 %all-to-all-done.2 = bf16[2,192,2048]{2,0,1:T(2,128)(2,1)S(1)} async-done(((bf16[2,192,2048]{2,0,1:T(2,128)(2,1)}), bf16[2,192,2048]{2,0,1:T(2,128)(2,1)S(1)}, u32[]{:S(2)}, u32[]{:S(2)}) %all-to-all-start.2) | async-done | bytes 1572896 | tf_op jit(solution)/shard_map/all_to_all | solution.py:125
  (103 shorter events, 66.3 us)
Async XLA Ops:
  6.5 66.2 %all-gather.5.cloned.1.call-start = ((), (), s32[]{:S(2)}) async-start(), calls=%async_computation.5 | async-start | bytes 3538944 | tf_op jit(solution)/shard_map/all_gather | solution.py:58
  7.3 126.8 %all-gather.7.cloned.1.call-start = ((), (), s32[]{:S(2)}) async-start(), calls=%async_computation.6 | async-start | bytes 3538944 | tf_op jit(solution)/shard_map/all_gather | solution.py:59
  8.0 335.4 %all-gather.9.cloned.1.call-start = ((), (), s32[]{:S(2)}) async-start(), calls=%async_computation.7 | async-start | bytes 14155776 | tf_op jit(solution)/shard_map/all_gather | solution.py:111
  76.8 2.1 copy-start
  78.9 59.8 %copy-start.2 = (f32[12,8,16,128]{3,2,1,0:T(8,128)S(1)}, f32[12,8,16,128]{3,2,1,0:T(8,128)}, u32[]{:S(2)}) copy-start(f32[12,8,16,128]{3,2,1,0:T(8,128)} %copy.93) | copy-start | bytes 2359300
  138.7 5.5 copy-start.1
  138.8 5.5 copy-start.3
  169.6 16.6 %all-to-all-start = ((s32[4,2,48]{2,1,0:T(2,128)}), s32[4,2,48]{2,1,0:T(2,128)S(1)}, u32[]{:S(2)}, u32[]{:S(2)}) async-start(s32[4,2,48]{2,1,0:T(2,128)} %all_to_all.38), calls=%async_computation | async-start | bytes 8192 | tf_op jit(solution)/shard_map/all_to_all | solution.py:108
  172.9 453.8 %reduce-scatter.3.cloned.1.call-start = ((), (), s32[]{:S(2)}) async-start(), calls=%async_computation.8 | async-start | bytes 7077888 | tf_op jit(solution)/shard_map/reduce_scatter | solution.py:120
  413.6 333.7 %reduce-scatter.5.cloned.1.call-start = ((), (), s32[]{:S(2)}) async-start(), calls=%async_computation.9 | async-start | bytes 7077888 | tf_op jit(solution)/shard_map/reduce_scatter | solution.py:120
  747.3 7.9 %copy-start.4 = (f32[1,96,2]{1,2,0:T(2,128)S(1)}, f32[1,96,2]{1,2,0:T(2,128)}, u32[]{:S(2)}) copy-start(f32[1,96,2]{1,2,0:T(2,128)} %param.21) | copy-start | bytes 2308
  751.6 23.6 %all-to-all-start.2 = ((bf16[2,192,2048]{2,0,1:T(2,128)(2,1)}), bf16[2,192,2048]{2,0,1:T(2,128)(2,1)S(1)}, u32[]{:S(2)}, u32[]{:S(2)}) async-start(bf16[2,192,2048]{2,0,1:T(2,128)(2,1)} %copy.86), calls=%async_computation.4 | async-start | bytes 3145728 | tf_op jit(solution)/shard_map/all_to_all | solution.py:125
Sparse Core Ops, SparseCore 0:
  9.5 63.1 all-gather.4
  74.9 59.0 all-gather.6
  169.0 174.3 all-gather.8
  413.7 212.9 reduce-scatter.2
  630.2 117.1 reduce-scatter.4
where the time goes:
time: 786 us; the launch traced here: 784 us
  waiting for transfers between devices  500 us (64%)
  local copies, waits for them, and re-layouts  136 us (17%)
  matrix products  53.8 us (7%)
  blocking collectives  49.4 us (6%)
  other arithmetic  22.8 us (3%)
  between operations  14.6 us (2%)
    reduce_scatter x2, waiting for transfers between devices, on_device(): lax.psum_scatter(partial_value, 'ctx', scatter_dimension=0, tiled=True)  245 us
    all_gather x1, waiting for transfers between devices, on_device(): lax.all_gather(arrived, 'ctx', axis=1, tiled=True)  121 us
    all_gather x1, waiting for transfers between devices, on_device(): key_piece = lax.all_gather(keys, 'ctx', axis=1, tiled=True)  58.6 us
    all_gather x1, waiting for transfers between devices, on_device(): value_piece = lax.all_gather(values, 'ctx', axis=1, tiled=True)  54 us
    dot_general x8, matrix products, one_block(): jnp.dot(inner_act, second_w, preferred_element_type=jnp.float32)  46.2 us
    gather x8, local copies, waits for them, and re-layouts, one_block(): inputs = jnp.take(gathered, picked, axis=0)  40.3 us
    gather x2, local copies, waits for them, and re-layouts, expert_partial(): unpacked = jnp.take(packed, back_idx, axis=0)  32.6 us
    all_gather x1, blocking collectives, on_device(): lax.all_gather(arrived_flags, 'ctx', axis=1, tiled=True)  26.8 us
  transfers between devices with their start and end apart: 7, of which 6 were waited for; matrix products, arithmetic and copies ran while one was open for 15% of the time, Pallas kernels for 0%

commit v1 on v0

--- a/solution.py
+++ b/solution.py
@@ -1,8 +1,11 @@
+import functools
 import math
 
 import jax
 import jax.numpy as jnp
 from jax import lax
+from jax.experimental import pallas as pl
+from jax.experimental.pallas import tpu as pltpu
 from jax.sharding import PartitionSpec as P
 
 HEADS = 16
@@ -49,39 +52,8 @@
     return jnp.where((live_flags > 0)[:, None], unpacked, jnp.zeros_like(unpacked))
 
 
-def on_device(frames, queries, keys, values, expert_ids, gate_weights, w_in, w_out):
-    tok_count = frames.shape[1]
-    model_width = frames.shape[2]
-    factor = 1.0 / math.sqrt(HD)
-    query_heads = queries[0].reshape(tok_count, HEADS, HD)
-    top_prev = jnp.full((HEADS, tok_count), -1e30, jnp.float32)
-    key_piece = lax.all_gather(keys, "ctx", axis=1, tiled=True)
-    value_piece = lax.all_gather(values, "ctx", axis=1, tiled=True)
-    piece_len = key_piece.shape[1]
-    key_heads = key_piece[0].reshape(piece_len, HEADS, HD)
-    value_heads = value_piece[0].reshape(piece_len, HEADS, HD)
-    scores = (
-        jnp.einsum("qhd,khd->hqk", query_heads, key_heads, preferred_element_type=jnp.float32)
-        * factor
-    )
-    top_next = jnp.maximum(top_prev, jnp.max(scores, axis=-1))
-    weights_raw = jnp.exp(scores - top_next[..., None])
-    total_next = jnp.sum(weights_raw, axis=-1)
-    accum = jnp.einsum(
-        "hqk,khd->hqd",
-        weights_raw.astype(jnp.bfloat16),
-        value_heads,
-        preferred_element_type=jnp.float32,
-    )
-    top_final, total_final, accum = (top_next, total_next, accum)
-    attended = jnp.transpose(accum / total_final[..., None], (1, 0, 2)).reshape(
-        tok_count, HEADS * HD
-    )
-    hidden_state = (frames[0].astype(jnp.float32) + attended).astype(jnp.bfloat16)
-    hidden_f = hidden_state.astype(jnp.float32)
-    normed = (
-        hidden_f * lax.rsqrt(jnp.mean(hidden_f * hidden_f, axis=-1, keepdims=True) + EPSILON)
-    ).astype(jnp.bfloat16)
+def routed_ffn(hidden_f, normed, expert_ids, gate_weights, w_in, w_out):
+    tok_count, model_width = normed.shape
     slot_ids = expert_ids[0].reshape(-1)
     slot_count = slot_ids.shape[0]
     exp_local = w_in.shape[0]
@@ -91,11 +63,9 @@
         jnp.int32
     )
     slot_rank = jnp.sum((jnp.cumsum(onehot, axis=0) - onehot) * onehot, axis=1)
-    sending = jnp.ones((slot_count,), bool)
     target = slot_ids * capacity + slot_rank
     send_matrix = (
-        (jnp.arange(num_experts * capacity, dtype=jnp.int32)[:, None] == target[None, :])
-        & sending[None, :]
+        jnp.arange(num_experts * capacity, dtype=jnp.int32)[:, None] == target[None, :]
     ).astype(jnp.int32)
     token_matrix = send_matrix.reshape(num_experts * capacity, tok_count, 2).sum(-1)
     outgoing = jnp.dot(
@@ -130,22 +100,210 @@
     )
     tok_out = slot_out.reshape(tok_count, 2, model_width)
     gates = gate_weights[0]
-    layer_out = hidden_f + gates[:, 0:1] * tok_out[:, 0] + gates[:, 1:2] * tok_out[:, 1]
+    return hidden_f + gates[:, 0:1] * tok_out[:, 0] + gates[:, 1:2] * tok_out[:, 1]
+
+
+def attend_kernel(q_ref, k_ref, v_ref, o_ref):
+    scores = lax.dot_general(
+        q_ref[...], k_ref[...], (((1,), (1,)), ((), ())), preferred_element_type=jnp.float32
+    ) * (1.0 / math.sqrt(HD))
+    raw = jnp.exp(scores - jnp.max(scores, axis=-1, keepdims=True))
+    total = jnp.sum(raw, axis=-1, keepdims=True)
+    mixed = jnp.dot(raw.astype(jnp.bfloat16), v_ref[...], preferred_element_type=jnp.float32)
+    o_ref[...] = (mixed / total).astype(o_ref.dtype)
+
+
+def attend_heads(packed, local_heads):
+    frames = packed.shape[0]
+    rows = 256
+    return pl.pallas_call(
+        attend_kernel,
+        grid=(local_heads, frames // rows),
+        in_specs=[
+            pl.BlockSpec((rows, HD), lambda h, i: (i, h)),
+            pl.BlockSpec((frames, HD), lambda h, i: (0, local_heads + h)),
+            pl.BlockSpec((frames, HD), lambda h, i: (0, 2 * local_heads + h)),
+        ],
+        out_specs=pl.BlockSpec((rows, HD), lambda h, i: (i, h)),
+        out_shape=jax.ShapeDtypeStruct((frames, local_heads * HD), jnp.bfloat16),
+        cost_estimate=pl.CostEstimate(
+            flops=4 * local_heads * frames * frames * HD,
+            bytes_accessed=8 * frames * local_heads * HD,
+            transcendentals=local_heads * frames * frames,
+        ),
+        name="attend_heads",
+    )(packed, packed, packed)
+
+
+def attention(queries, keys, values):
+    n_ctx = lax.axis_size("ctx")
+    tok_count, width = queries.shape
+    local_heads = HEADS // n_ctx
+    piece = width // n_ctx
+    outgoing = jnp.concatenate(
+        [jnp.transpose(a.reshape(tok_count, n_ctx, piece), (1, 0, 2)) for a in (queries, keys, values)],
+        axis=-1,
+    )
+    arrived = lax.all_to_all(outgoing, "ctx", split_axis=0, concat_axis=0, tiled=True)
+    mixed = attend_heads(arrived.reshape(n_ctx * tok_count, 3 * piece), local_heads)
+    returned = lax.all_to_all(
+        mixed.reshape(n_ctx, tok_count, piece), "ctx", split_axis=0, concat_axis=0, tiled=True
+    )
+    return jnp.transpose(returned, (1, 0, 2)).reshape(tok_count, width)
+
+
+def swap_core(a):
+    return lax.ppermute(a, "exp", [(i, i ^ 1) for i in range(4)])
+
+
+def swap_x(a):
+    return lax.ppermute(a, "exp", [(i, i ^ 2) for i in range(4)])
+
+
+def swap_y(a):
+    return lax.ppermute(a, "ctx", [(i, i ^ 1) for i in range(8)])
+
+
+def turn_z(a, steps):
+    return lax.ppermute(a, "ctx", [(i, (i + 2 * steps) % 8) for i in range(8)])
+
+
+def ffn_kernel(*refs, n_parts):
+    parts = refs[:n_parts]
+    gate_ref, first_ref, second_ref, own_ref, other_ref, rows_ref, total_ref = refs[n_parts:]
+    expert, block = pl.program_id(0), pl.program_id(1)
+    first_step = (expert == 0) & (block == 0)
+    last_step = (expert == pl.num_programs(0) - 1) & (block == pl.num_programs(1) - 1)
+
+    @pl.when(first_step)
+    def _():
+        at = 0
+        for part in parts:
+            size = part.shape[0]
+            rows_ref[at : at + size, :] = part[...]
+            at += size
+
+    inner = gelu_tanh(
+        jnp.dot(rows_ref[...], first_ref[0], preferred_element_type=jnp.float32)
+    ) * gate_ref[0]
+    product = jnp.dot(
+        inner.astype(jnp.bfloat16), second_ref[0], preferred_element_type=jnp.float32
+    )
+
+    @pl.when(first_step)
+    def _():
+        total_ref[...] = product
+
+    @pl.when(jnp.logical_not(first_step))
+    def _():
+        total_ref[...] += product
+
+    @pl.when(last_step)
+    def _():
+        half = own_ref.shape[0]
+        own_ref[...] = total_ref[:half].astype(own_ref.dtype)
+        other_ref[...] = total_ref[half:].astype(other_ref.dtype)
+
+
+def dense_ffn(parts, gate, w_in, w_out):
+    rows = sum(p.shape[0] for p in parts)
+    n_exp, width, inner = w_in.shape
+    cut = 512
+    whole = lambda e, f: (0, 0)
+    half = jax.ShapeDtypeStruct((rows // 2, width), jnp.bfloat16)
+    return pl.pallas_call(
+        functools.partial(ffn_kernel, n_parts=len(parts)),
+        grid=(n_exp, inner // cut),
+        in_specs=[pl.BlockSpec(p.shape, whole, pipeline_mode=pl.Buffered(1)) for p in parts]
+        + [
+            pl.BlockSpec((1, rows, 1), lambda e, f: (e, 0, 0)),
+            pl.BlockSpec((1, width, cut), lambda e, f: (e, 0, f)),
+            pl.BlockSpec((1, cut, width), lambda e, f: (e, f, 0)),
+        ],
+        out_specs=[pl.BlockSpec(half.shape, whole)] * 2,
+        out_shape=[half, half],
+        scratch_shapes=[
+            pltpu.VMEM((rows, width), jnp.bfloat16),
+            pltpu.VMEM((rows, width), jnp.float32),
+        ],
+        compiler_params=pltpu.CompilerParams(vmem_limit_bytes=56 << 20),
+        cost_estimate=pl.CostEstimate(
+            flops=4 * n_exp * rows * width * inner,
+            bytes_accessed=4 * n_exp * width * inner + 4 * rows * width,
+            transcendentals=n_exp * rows * inner,
+        ),
+        name="dense_ffn",
+    )(*parts, gate, w_in, w_out)
+
+
+def gather_plane(a):
+    half = a.shape[0] // 2
+    by_y, by_x = swap_y(a), swap_x(a)
+    corner_x, corner_y = swap_x(by_y[:half]), swap_y(by_x[half:])
+    mine = [a, by_y, by_x, corner_x, corner_y]
+    return mine + [swap_core(p) for p in mine]
+
+
+def reduce_plane(own_half, other_half, tok_count):
+    half = tok_count // 2
+    both = own_half.astype(jnp.float32) + swap_core(other_half).astype(jnp.float32)
+    mine, to_y, to_x = (both[i * tok_count : (i + 1) * tok_count] for i in range(3))
+    corner = both[3 * tok_count :].astype(jnp.bfloat16)
+    from_x, from_y = swap_x(corner[:half]), swap_y(corner[half:])
+    to_y = to_y.at[:half].add(from_x.astype(jnp.float32)).astype(jnp.bfloat16)
+    to_x = to_x.at[half:].add(from_y.astype(jnp.float32)).astype(jnp.bfloat16)
+    return mine + swap_y(to_y).astype(jnp.float32) + swap_x(to_x).astype(jnp.float32)
+
+
+def dense_sum(hidden_f, normed, expert_ids, gate_weights, w_in, w_out):
+    tok_count, _ = normed.shape
+    n_local = w_in.shape[0]
+    small = jnp.concatenate([expert_ids[0].astype(jnp.float32).T, gate_weights[0].T], axis=0)
+    by_y = swap_y(small)
+    small = jnp.stack([small, by_y])
+    small = jnp.concatenate([small, swap_x(small)])
+    small = jnp.concatenate([small, swap_core(small)])
+    small = [small] + [turn_z(small, k) for k in range(1, 4)]
+    local_ids = (
+        lax.axis_index("exp") * n_local + jnp.arange(n_local, dtype=jnp.int32)
+    ).astype(jnp.float32)
+
+    gathered, ring = [], normed
+    for k in range(4):
+        if k:
+            ring = turn_z(ring, 1)
+        gathered.append(gather_plane(ring))
+    total = hidden_f
+    for k in range(4):
+        ids = jnp.transpose(small[k][:, 0:2], (1, 0, 2)).reshape(2, -1)
+        gates = jnp.transpose(small[k][:, 2:4], (1, 0, 2)).reshape(2, -1)
+        gate = jnp.sum(
+            jnp.where(ids[None] == local_ids[:, None, None], gates[None], 0.0), axis=1
+        )
+        own_half, other_half = dense_ffn(gathered[k], gate[..., None], w_in, w_out)
+        plane = reduce_plane(own_half, other_half, tok_count)
+        if k:
+            plane = turn_z(plane.astype(jnp.bfloat16), -k).astype(jnp.float32)
+        total = total + plane
+    return total
+
+
+def on_device(frames, queries, keys, values, expert_ids, gate_weights, w_in, w_out):
+    attended = attention(queries[0], keys[0], values[0]).astype(jnp.float32)
+    hidden_state = (frames[0].astype(jnp.float32) + attended).astype(jnp.bfloat16)
+    hidden_f = hidden_state.astype(jnp.float32)
+    normed = (
+        hidden_f * lax.rsqrt(jnp.mean(hidden_f * hidden_f, axis=-1, keepdims=True) + EPSILON)
+    ).astype(jnp.bfloat16)
+    dense = lax.axis_size("ctx") == 8 and lax.axis_size("exp") == 4
+    ffn = dense_sum if dense else routed_ffn
+    layer_out = ffn(hidden_f, normed, expert_ids, gate_weights, w_in, w_out)
     return layer_out.astype(jnp.bfloat16)[None]
 
 
 def solution(mesh):
-    in_specs = (
-        P("exp", "ctx", None),
-        P("exp", "ctx", None),
-        P("exp", "ctx", None),
-        P("exp", "ctx", None),
-        P("exp", "ctx", None),
-        P("exp", "ctx", None),
-        P("exp", None, "ctx"),
-        P("exp", "ctx", None),
-    )
-    out_specs = P("exp", "ctx", None)
+    rows = P("exp", "ctx", None)
+    in_specs = (rows,) * 6 + (P("exp", None, "ctx"), P("exp", "ctx", None))
     return jax.shard_map(
-        on_device, mesh=mesh, in_specs=in_specs, out_specs=out_specs, check_vma=False
-    )
+        on_device, mesh=mesh, in_specs=in_specs, out_specs=rows, check_vma=False
+    )

time: 786 us -> 325 us (0.41)
  waiting for transfers between devices: 500 us -> 94 us
  local copies, waits for them, and re-layouts: 136 us -> 13.2 us
  Pallas kernels: 0 us -> 99.6 us
  matrix products: 53.8 us -> 0 us
  starting transfers between devices: 6.97 us -> 60.5 us
  other arithmetic: 22.8 us -> 5.37 us
  between operations: 14.6 us -> 0.67 us
    reduce_scatter x2 -> x0, waiting for transfers between devices: 245 us -> none  [on_device(): lax.psum_scatter(partial_value, 'ctx', scatter_dimension=0, tiled=True)]
    all_gather x3 -> x0, waiting for transfers between devices: 234 us -> none  [the longest x1 121 us: on_device(): lax.all_gather(arrived, 'ctx', axis=1, tiled=True)]
    pallas_call x0 -> x5, Pallas kernels: none -> 99.6 us  [the longest x4 93.3 us: dense_ffn(): pl.pallas_call(functools.partial(ffn_kernel, n_parts=len(parts)), grid=(n...]
    ppermute x0 -> x68, waiting for transfers between devices: none -> 94 us  [the longest x17 35.6 us: swap_y(): return lax.ppermute(a, 'ctx', [(i, i ^ 1) for i in range(8)])]
    gather x10 -> x0, local copies, waits for them, and re-layouts: 72.8 us -> none  [the longest x8 40.3 us: one_block(): inputs = jnp.take(gathered, picked, axis=0)]
    ppermute x0 -> x68, starting transfers between devices: none -> 60.5 us  [the longest x17 20.4 us: swap_y(): return lax.ppermute(a, 'ctx', [(i, i ^ 1) for i in range(8)])]
    dot_general x12 -> x0, matrix products: 53.8 us -> none  [the longest x8 46.2 us: one_block(): jnp.dot(inner_act, second_w, preferred_element_type=jnp.float32)]
    all_to_all x1 -> x2, blocking collectives: 22.6 us -> 51.3 us  [the longest x1 36.1 us: attention(): lax.all_to_all(outgoing, 'ctx', split_axis=0, concat_axis=0, tiled=True)]
  transfers between devices with their start and end apart: 7 -> 68, of which waited for: 6 -> 22; matrix products, arithmetic and copies ran while one was open for 15% -> 4% of each run, Pallas kernels for 0% -> 29%
where the time goes in v1:
time: 325 us
  Pallas kernels  99.6 us (31%)
  waiting for transfers between devices  94 us (29%)
  starting transfers between devices  60.5 us (19%)
  blocking collectives  51.3 us (16%)
  local copies, waits for them, and re-layouts  13.2 us (4%)
  other arithmetic  5.37 us (2%)
    pallas_call x4, Pallas kernels, dense_ffn(): pl.pallas_call(functools.partial(ffn_kernel, n_parts=len(parts)), grid=(n...  93.3 us
    all_to_all x1, blocking collectives, attention(): lax.all_to_all(outgoing, 'ctx', split_axis=0, concat_axis=0, tiled=True)  36.1 us
    ppermute x17, waiting for transfers between devices, swap_y(): return lax.ppermute(a, 'ctx', [(i, i ^ 1) for i in range(8)])  35.6 us
    ppermute x17, waiting for transfers between devices, swap_x(): return lax.ppermute(a, 'exp', [(i, i ^ 2) for i in range(4)])  34.9 us
    ppermute x9, waiting for transfers between devices, turn_z(): return lax.ppermute(a, 'ctx', [(i, (i + 2 * steps) % 8) for i in range(8)])  22.5 us
    ppermute x17, starting transfers between devices, swap_y(): return lax.ppermute(a, 'ctx', [(i, i ^ 1) for i in range(8)])  20.4 us
    ppermute x17, starting transfers between devices, swap_x(): return lax.ppermute(a, 'exp', [(i, i ^ 2) for i in range(4)])  20.3 us
    all_to_all x1, blocking collectives, attention(): lax.all_to_all(mixed.reshape(n_ctx, tok_count, piece), 'ctx', split_axis=...  15.1 us
  transfers between devices with their start and end apart: 68, of which 22 were waited for; matrix products, arithmetic and copies ran while one was open for 4% of the time, Pallas kernels for 29%

profile of v1, /device:TPU:0, one launch (start us, length us, event | category | flops | bytes accessed | tf_op | source)
XLA Modules:
  0.0 324.6 jit_solution(12150498690954819824)
XLA Ops:
  2.6 36.1 %all_to_all.10 = bf16[8,96,768]{2,1,0:T(8,128)(2,1)} all-to-all(bf16[8,96,768]{2,1,0:T(8,128)(2,1)S(1)} %pad_maximum_fusion), channel_id=1, replica_groups=mesh['ctx'=8,'exp'=4] {'ctx'}, dimensions={0} | all-to-all | bytes 2359296 | tf_op jit(solution)/shard_map/all_to_all | solution.py:147
  38.8 6.3 %attend_heads.1 = bf16[768,256]{1,0:T(8,128)(2,1)} custom-call(bf16[768,768]{1,0:T(8,128)(2,1)} %bitcast.58, bf16[768,768]{1,0:T(8,128)(2,1)} %bitcast.59, bf16[768,768]{1,0:T(8,128)(2,1)} %bitcast.60), custom_call_target="tpu_custom_call" | custom-call | flops 603979776 | bytes 1572864 | tf_op jit(solution)/shard_map/attend_heads/pallas_call | solution.py:119
  45.1 15.1 %all_to_all.11 = bf16[8,96,256]{2,1,0:T(8,128)(2,1)S(1)} all-to-all(bf16[8,96,256]{2,1,0:T(8,128)(2,1)} %bitcast.66), channel_id=1, replica_groups=mesh['ctx'=8,'exp'=4] {'ctx'}, dimensions={0} | all-to-all | bytes 786432 | tf_op jit(solution)/shard_map/all_to_all | solution.py:149
  66.1 4.4 %collective-permute-done.9 = f32[4,96]{1,0:T(4,128)S(1)} collective-permute-done((f32[4,96]{1,0:T(4,128)S(1)}, f32[4,96]{1,0:T(4,128)S(1)}, u32[]{:S(2)}, u32[]{:S(2)}) %collective-permute-start.9) | collective-permute-done | bytes 1568 | tf_op jit(solution)/shard_map/ppermute | solution.py:164
  72.1 2.2 collective-permute-start.34
  75.6 2.0 collective-permute-start.27
  77.6 1.8 collective-permute-start.44
  80.9 5.3 %collective-permute-done.27 = f32[8,4,96]{2,1,0:T(4,128)S(1)} collective-permute-done((f32[8,4,96]{2,1,0:T(4,128)S(1)}, f32[8,4,96]{2,1,0:T(4,128)S(1)}, u32[]{:S(2)}, u32[]{:S(2)}) %collective-permute-start.27) | collective-permute-done | bytes 12320 | tf_op jit(solution)/shard_map/ppermute | solution.py:168
  90.3 3.9 %collective-permute-done.2.refs_3_ = bf16[48,2048]{1,0:T(8,128)(2,1)} collective-permute-done((bf16[48,2048]{1,0:T(8,128)(2,1)S(1)}, bf16[48,2048]{1,0:T(8,128)(2,1)}, u32[]{:S(2)}, u32[]{:S(2)}) %collective-permute-start.2) | collective-permute-done | bytes 196640 | tf_op jit(solution)/shard_map/ppermute | solution.py:160
  95.2 6.6 %collective-permute-done.18.refs_1_ = bf16[96,2048]{1,0:T(8,128)(2,1)S(1)} collective-permute-done((bf16[96,2048]{1,0:T(8,128)(2,1)S(1)}, bf16[96,2048]{1,0:T(8,128)(2,1)S(1)}, u32[]{:S(2)}, u32[]{:S(2)}) %collective-permute-start.18) | collective-permute-done | bytes 393248 | tf_op jit(solution)/shard_map/ppermute | solution.py:164
  107.2 3.1 collective-permute-done.20.refs_3_
  110.3 8.3 %collective-permute-done.21.refs_4_ = bf16[48,2048]{1,0:T(8,128)(2,1)S(1)} collective-permute-done((bf16[48,2048]{1,0:T(8,128)(2,1)S(1)}, bf16[48,2048]{1,0:T(8,128)(2,1)S(1)}, u32[]{:S(2)}, u32[]{:S(2)}) %collective-permute-start.21) | collective-permute-done | bytes 196640 | tf_op jit(solution)/shard_map/ppermute | solution.py:164
  132.0 23.2 %dense_ffn.4 = (bf16[384,2048]{1,0:T(8,128)(2,1)}, bf16[384,2048]{1,0:T(8,128)(2,1)}) custom-call(bf16[96,2048]{1,0:T(8,128)(2,1)} %copy-done.6, bf16[96,2048]{1,0:T(8,128)(2,1)} %copy-done.7, bf16[96,2048]{1,0:T(8,128)(2,1)} %copy-done.8, bf16[48,2048]{1,0:T(8,128)(2,1)} %collective-permute-done.2.refs_3_, bf16[48,2048]{1,0:T(8,128)(2,1)} %collective-permute-done.3.refs_4_, ...), custom_call_target="tpu_custom_call" | custom-call | flops 12884901888 | bytes 23068672 | tf_op jit(solution)/shard_map/dense_ffn/pallas_call | solution.py:214
  158.2 2.0 collective-permute-start.54
  160.5 23.2 %dense_ffn.5 = (bf16[384,2048]{1,0:T(8,128)(2,1)}, bf16[384,2048]{1,0:T(8,128)(2,1)}) custom-call(bf16[96,2048]{1,0:T(8,128)(2,1)} %copy-done.16, bf16[96,2048]{1,0:T(8,128)(2,1)} %copy-done.9, bf16[96,2048]{1,0:T(8,128)(2,1)} %copy-done.10, bf16[48,2048]{1,0:T(8,128)(2,1)} %collective-permute-done.20.refs_3_, bf16[48,2048]{1,0:T(8,128)(2,1)} %copy-done.24, ...), custom_call_target="tpu_custom_call" | custom-call | flops 12884901888 | bytes 23068672 | tf_op jit(solution)/shard_map/dense_ffn/pallas_call | solution.py:214
  185.0 23.5 %dense_ffn.6 = (bf16[384,2048]{1,0:T(8,128)(2,1)}, bf16[384,2048]{1,0:T(8,128)(2,1)}) custom-call(bf16[96,2048]{1,0:T(8,128)(2,1)} %collective-permute-done.34.refs_0_, bf16[96,2048]{1,0:T(8,128)(2,1)} %copy-done.11, bf16[96,2048]{1,0:T(8,128)(2,1)} %copy-done.12, bf16[48,2048]{1,0:T(8,128)(2,1)} %copy-done.26, bf16[48,2048]{1,0:T(8,128)(2,1)} %copy-done.27, ...), custom_call_target="tpu_custom_call" | custom-call | flops 12884901888 | bytes 23068672 | tf_op jit(solution)/shard_map/dense_ffn/pallas_call | solution.py:214
  210.5 23.3 %dense_ffn.7 = (bf16[384,2048]{1,0:T(8,128)(2,1)}, bf16[384,2048]{1,0:T(8,128)(2,1)}) custom-call(bf16[96,2048]{1,0:T(8,128)(2,1)} %collective-permute-done.51.refs_0_, bf16[96,2048]{1,0:T(8,128)(2,1)} %collective-permute-done.52.refs_1_, bf16[96,2048]{1,0:T(8,128)(2,1)} %collective-permute-done.53.refs_2_, ...), custom_call_target="tpu_custom_call" | custom-call | flops 12884901888 | bytes 23068672 | tf_op jit(solution)/shard_map/dense_ffn/pallas_call | solution.py:214
  236.7 5.3 %collective-permute-done.13 = bf16[48,2048]{1,0:T(8,128)(2,1)S(1)} collective-permute-done((bf16[48,2048]{1,0:T(8,128)(2,1)S(1)}, bf16[48,2048]{1,0:T(8,128)(2,1)S(1)}, u32[]{:S(2)}, u32[]{:S(2)}) %collective-permute-start.13) | collective-permute-done | bytes 196640 | tf_op jit(solution)/shard_map/ppermute | solution.py:160
  246.8 10.1 %collective-permute-done.29 = bf16[48,2048]{1,0:T(8,128)(2,1)S(1)} collective-permute-done((bf16[48,2048]{1,0:T(8,128)(2,1)S(1)}, bf16[48,2048]{1,0:T(8,128)(2,1)S(1)}, u32[]{:S(2)}, u32[]{:S(2)}) %collective-permute-start.29) | collective-permute-done | bytes 196640 | tf_op jit(solution)/shard_map/ppermute | solution.py:160
  256.9 1.8 collective-permute-start.14
  261.3 3.9 %collective-permute-done.46 = bf16[48,2048]{1,0:T(8,128)(2,1)S(1)} collective-permute-done((bf16[48,2048]{1,0:T(8,128)(2,1)S(1)}, bf16[48,2048]{1,0:T(8,128)(2,1)S(1)}, u32[]{:S(2)}, u32[]{:S(2)}) %collective-permute-start.46) | collective-permute-done | bytes 196640 | tf_op jit(solution)/shard_map/ppermute | solution.py:160
  266.7 4.1 %collective-permute-done.48 = bf16[48,2048]{1,0:T(8,128)(2,1)S(1)} collective-permute-done((bf16[48,2048]{1,0:T(8,128)(2,1)S(1)}, bf16[48,2048]{1,0:T(8,128)(2,1)S(1)}, u32[]{:S(2)}, u32[]{:S(2)}) %collective-permute-start.48) | collective-permute-done | bytes 196640 | tf_op jit(solution)/shard_map/ppermute | solution.py:164
  270.8 1.7 collective-permute-start.30
  272.6 1.8 collective-permute-done.32
  276.0 3.5 %collective-permute-done.30 = bf16[96,2048]{1,0:T(8,128)(2,1)S(1)} collective-permute-done((bf16[96,2048]{1,0:T(8,128)(2,1)S(1)}, bf16[96,2048]{1,0:T(8,128)(2,1)S(1)}, u32[]{:S(2)}, u32[]{:S(2)}) %collective-permute-start.30) | collective-permute-done | bytes 393248 | tf_op jit(solution)/shard_map/ppermute | solution.py:164
  283.1 3.4 %collective-permute-done.63 = bf16[48,2048]{1,0:T(8,128)(2,1)S(1)} collective-permute-done((bf16[48,2048]{1,0:T(8,128)(2,1)S(1)}, bf16[48,2048]{1,0:T(8,128)(2,1)S(1)}, u32[]{:S(2)}, u32[]{:S(2)}) %collective-permute-start.63) | collective-permute-done | bytes 196640 | tf_op jit(solution)/shard_map/ppermute | solution.py:160
  288.0 3.5 %collective-permute-start.33 = (bf16[96,2048]{1,0:T(8,128)(2,1)S(1)}, bf16[96,2048]{1,0:T(8,128)(2,1)S(1)}, u32[]{:S(2)}, u32[]{:S(2)}) collective-permute-start(bf16[96,2048]{1,0:T(8,128)(2,1)S(1)} %fusion.11), channel_id=1, source_target_pairs={{0,24},{4,28},{8,0},{12,4},{16,8},{20,12},{24,16},{28,20},{1,25},{... | collective-permute-start | bytes 1179656 | tf_op jit(solution)/shard_map/ppermute | solution.py:168
  292.8 2.8 collective-permute-done.47
  297.4 2.0 collective-permute-done.66
  299.4 4.5 %collective-permute-done.64 = bf16[96,2048]{1,0:T(8,128)(2,1)S(1)} collective-permute-done((bf16[96,2048]{1,0:T(8,128)(2,1)S(1)}, bf16[96,2048]{1,0:T(8,128)(2,1)S(1)}, u32[]{:S(2)}, u32[]{:S(2)}) %collective-permute-start.64) | collective-permute-done | bytes 393248 | tf_op jit(solution)/shard_map/ppermute | solution.py:164
  304.0 2.2 collective-permute-start.67
  306.2 17.2 %collective-permute-done.50 = bf16[96,2048]{1,0:T(8,128)(2,1)S(1)} collective-permute-done((bf16[96,2048]{1,0:T(8,128)(2,1)S(1)}, bf16[96,2048]{1,0:T(8,128)(2,1)S(1)}, u32[]{:S(2)}, u32[]{:S(2)}) %collective-permute-start.50) | collective-permute-done | bytes 393248 | tf_op jit(solution)/shard_map/ppermute | solution.py:168
  (243 shorter events, 65.8 us)
Async XLA Ops:
  62.5 15.1 %collective-permute-start = (bf16[96,2048]{1,0:T(8,128)(2,1)S(1)}, bf16[96,2048]{1,0:T(8,128)(2,1)S(1)}, u32[]{:S(2)}, u32[]{:S(2)}) collective-permute-start(bf16[96,2048]{1,0:T(8,128)(2,1)S(1)} %fusion.1.refs_0_), channel_id=1, source_target_pairs={{0,4},{4,0},{8,12},{12,8},{16,20},{20,16},{24,28},{28,24},{1,5},{5... | collective-permute-start | bytes 1179656 | tf_op jit(solution)/shard_map/ppermute | solution.py:164
  62.9 16.5 %collective-permute-start.1 = (bf16[96,2048]{1,0:T(8,128)(2,1)S(1)}, bf16[96,2048]{1,0:T(8,128)(2,1)S(1)}, u32[]{:S(2)}, u32[]{:S(2)}) collective-permute-start(bf16[96,2048]{1,0:T(8,128)(2,1)S(1)} %fusion.1.refs_0_), channel_id=1, source_target_pairs={{0,2},{1,3},{2,0},{3,1},{4,6},{5,7},{6,4},{7,5},{8,10},{9,11},{10,... | collective-permute-start | bytes 1179656 | tf_op jit(solution)/shard_map/ppermute | solution.py:160
  72.1 16.7 %collective-permute-start.4 = (bf16[96,2048]{1,0:T(8,128)(2,1)S(1)}, bf16[96,2048]{1,0:T(8,128)(2,1)}, u32[]{:S(2)}, u32[]{:S(2)}) collective-permute-start(bf16[96,2048]{1,0:T(8,128)(2,1)S(1)} %fusion.1.refs_0_), channel_id=1, source_target_pairs={{0,1},{1,0},{2,3},{3,2},{4,5},{5,4},{6,7},{7,6},{8,9},{9,8},{10,11... | collective-permute-start | bytes 1179656 | tf_op jit(solution)/shard_map/ppermute | solution.py:156
  72.1 22.6 %collective-permute-start.34 = (bf16[96,2048]{1,0:T(8,128)(2,1)S(1)}, bf16[96,2048]{1,0:T(8,128)(2,1)}, u32[]{:S(2)}, u32[]{:S(2)}) collective-permute-start(bf16[96,2048]{1,0:T(8,128)(2,1)S(1)} %collective-permute-done.17.refs_0_), channel_id=1, source_target_pairs={{0,8},{4,12},{8,16},{12,20},{16,24},{20,28},{24,0},{28,4},{1,9},{5... | collective-permute-start | bytes 1179656 | tf_op jit(solution)/shard_map/ppermute | solution.py:168
  103.2 15.4 %collective-permute-start.51 = (bf16[96,2048]{1,0:T(8,128)(2,1)}, bf16[96,2048]{1,0:T(8,128)(2,1)}, u32[]{:S(2)}, u32[]{:S(2)}) collective-permute-start(bf16[96,2048]{1,0:T(8,128)(2,1)} %collective-permute-done.34.refs_0_), channel_id=1, source_target_pairs={{0,8},{4,12},{8,16},{12,20},{16,24},{20,28},{24,0},{28,4},{1,9},{5... | collective-permute-start | bytes 1179656 | tf_op jit(solution)/shard_map/ppermute | solution.py:168
  103.5 15.6 %collective-permute-start.35 = (bf16[96,2048]{1,0:T(8,128)(2,1)}, bf16[96,2048]{1,0:T(8,128)(2,1)S(1)}, u32[]{:S(2)}, u32[]{:S(2)}) collective-permute-start(bf16[96,2048]{1,0:T(8,128)(2,1)} %collective-permute-done.34.refs_0_), channel_id=1, source_target_pairs={{0,4},{4,0},{8,12},{12,8},{16,20},{20,16},{24,28},{28,24},{1,5},{5... | collective-permute-start | bytes 1179656 | tf_op jit(solution)/shard_map/ppermute | solution.py:164
  104.9 15.8 %collective-permute-start.36 = (bf16[96,2048]{1,0:T(8,128)(2,1)}, bf16[96,2048]{1,0:T(8,128)(2,1)S(1)}, u32[]{:S(2)}, u32[]{:S(2)}) collective-permute-start(bf16[96,2048]{1,0:T(8,128)(2,1)} %collective-permute-done.34.refs_0_), channel_id=1, source_target_pairs={{0,2},{1,3},{2,0},{3,1},{4,6},{5,7},{6,4},{7,5},{8,10},{9,11},{10,... | collective-permute-start | bytes 1179656 | tf_op jit(solution)/shard_map/ppermute | solution.py:160
  128.4 28.7 %collective-permute-start.26 = (bf16[48,2048]{1,0:T(8,128)(2,1)S(1)}, bf16[48,2048]{1,0:T(8,128)(2,1)S(1)}, u32[]{:S(2)}, u32[]{:S(2)}) collective-permute-start(bf16[48,2048]{1,0:T(8,128)(2,1)S(1)} %copy-done.25), channel_id=1, source_target_pairs={{0,1},{1,0},{2,3},{3,2},{4,5},{5,4},{6,7},{7,6},{8,9},{9,8},{10,11... | collective-permute-start | bytes 589832 | tf_op jit(solution)/shard_map/ppermute | solution.py:156
  128.5 29.2 %collective-permute-start.37 = (bf16[48,2048]{1,0:T(8,128)(2,1)S(1)}, bf16[48,2048]{1,0:T(8,128)(2,1)S(1)}, u32[]{:S(2)}, u32[]{:S(2)}) collective-permute-start(bf16[48,2048]{1,0:T(8,128)(2,1)S(1)} %slice.350), channel_id=1, source_target_pairs={{0,2},{1,3},{2,0},{3,1},{4,6},{5,7},{6,4},{7,5},{8,10},{9,11},{10,... | collective-permute-start | bytes 589832 | tf_op jit(solution)/shard_map/ppermute | solution.py:160
  129.2 28.5 %collective-permute-start.38 = (bf16[48,2048]{1,0:T(8,128)(2,1)S(1)}, bf16[48,2048]{1,0:T(8,128)(2,1)S(1)}, u32[]{:S(2)}, u32[]{:S(2)}) collective-permute-start(bf16[48,2048]{1,0:T(8,128)(2,1)S(1)} %slice.351), channel_id=1, source_target_pairs={{0,4},{4,0},{8,12},{12,8},{16,20},{20,16},{24,28},{28,24},{1,5},{5... | collective-permute-start | bytes 589832 | tf_op jit(solution)/shard_map/ppermute | solution.py:164
  130.5 27.7 %collective-permute-start.56 = (bf16[96,2048]{1,0:T(8,128)(2,1)}, bf16[96,2048]{1,0:T(8,128)(2,1)S(1)}, u32[]{:S(2)}, u32[]{:S(2)}) collective-permute-start(bf16[96,2048]{1,0:T(8,128)(2,1)} %collective-permute-done.51.refs_0_), channel_id=1, source_target_pairs={{0,1},{1,0},{2,3},{3,2},{4,5},{5,4},{6,7},{7,6},{8,9},{9,8},{10,11... | collective-permute-start | bytes 1179656 | tf_op jit(solution)/shard_map/ppermute | solution.py:156
  132.0 28.2 %collective-permute-start.40 = (bf16[96,2048]{1,0:T(8,128)(2,1)S(1)}, bf16[96,2048]{1,0:T(8,128)(2,1)S(1)}, u32[]{:S(2)}, u32[]{:S(2)}) collective-permute-start(bf16[96,2048]{1,0:T(8,128)(2,1)S(1)} %collective-permute-done.35.refs_1_), channel_id=1, source_target_pairs={{0,1},{1,0},{2,3},{3,2},{4,5},{5,4},{6,7},{7,6},{8,9},{9,8},{10,11... | collective-permute-start | bytes 1179656 | tf_op jit(solution)/shard_map/ppermute | solution.py:156
  157.1 26.6 %collective-permute-start.41 = (bf16[96,2048]{1,0:T(8,128)(2,1)S(1)}, bf16[96,2048]{1,0:T(8,128)(2,1)S(1)}, u32[]{:S(2)}, u32[]{:S(2)}) collective-permute-start(bf16[96,2048]{1,0:T(8,128)(2,1)S(1)} %collective-permute-done.36.refs_2_), channel_id=1, source_target_pairs={{0,1},{1,0},{2,3},{3,2},{4,5},{5,4},{6,7},{7,6},{8,9},{9,8},{10,11... | collective-permute-start | bytes 1179656 | tf_op jit(solution)/shard_map/ppermute | solution.py:156
  157.7 26.2 %collective-permute-start.42 = (bf16[48,2048]{1,0:T(8,128)(2,1)S(1)}, bf16[48,2048]{1,0:T(8,128)(2,1)S(1)}, u32[]{:S(2)}, u32[]{:S(2)}) collective-permute-start(bf16[48,2048]{1,0:T(8,128)(2,1)S(1)} %collective-permute-done.37.refs_3_), channel_id=1, source_target_pairs={{0,1},{1,0},{2,3},{3,2},{4,5},{5,4},{6,7},{7,6},{8,9},{9,8},{10,11... | collective-permute-start | bytes 589832 | tf_op jit(solution)/shard_map/ppermute | solution.py:156
  157.8 26.6 %collective-permute-start.43 = (bf16[48,2048]{1,0:T(8,128)(2,1)S(1)}, bf16[48,2048]{1,0:T(8,128)(2,1)S(1)}, u32[]{:S(2)}, u32[]{:S(2)}) collective-permute-start(bf16[48,2048]{1,0:T(8,128)(2,1)S(1)} %collective-permute-done.38.refs_4_), channel_id=1, source_target_pairs={{0,1},{1,0},{2,3},{3,2},{4,5},{5,4},{6,7},{7,6},{8,9},{9,8},{10,11... | collective-permute-start | bytes 589832 | tf_op jit(solution)/shard_map/ppermute | solution.py:156
  158.2 26.2 %collective-permute-start.54 = (bf16[48,2048]{1,0:T(8,128)(2,1)S(1)}, bf16[48,2048]{1,0:T(8,128)(2,1)}, u32[]{:S(2)}, u32[]{:S(2)}) collective-permute-start(bf16[48,2048]{1,0:T(8,128)(2,1)S(1)} %slice.361), channel_id=1, source_target_pairs={{0,2},{1,3},{2,0},{3,1},{4,6},{5,7},{6,4},{7,5},{8,10},{9,11},{10,... | collective-permute-start | bytes 589832 | tf_op jit(solution)/shard_map/ppermute | solution.py:160
  160.2 24.7 %collective-permute-start.55 = (bf16[48,2048]{1,0:T(8,128)(2,1)S(1)}, bf16[48,2048]{1,0:T(8,128)(2,1)}, u32[]{:S(2)}, u32[]{:S(2)}) collective-permute-start(bf16[48,2048]{1,0:T(8,128)(2,1)S(1)} %slice.362), channel_id=1, source_target_pairs={{0,4},{4,0},{8,12},{12,8},{16,20},{20,16},{24,28},{28,24},{1,5},{5... | collective-permute-start | bytes 589832 | tf_op jit(solution)/shard_map/ppermute | solution.py:164
  183.8 50.2 %collective-permute-start.12 = (bf16[384,2048]{1,0:T(8,128)(2,1)}, bf16[384,2048]{1,0:T(8,128)(2,1)S(1)}, u32[]{:S(2)}, u32[]{:S(2)}) collective-permute-start(bf16[384,2048]{1,0:T(8,128)(2,1)} %get-tuple-element.110), channel_id=1, source_target_pairs={{0,1},{1,0},{2,3},{3,2},{4,5},{5,4},{6,7},{7,6},{8,9},{9,8},{10,11... | collective-permute-start | bytes 4718600 | tf_op jit(solution)/shard_map/ppermute | solution.py:156
  183.9 24.7 %collective-permute-start.57 = (bf16[96,2048]{1,0:T(8,128)(2,1)}, bf16[96,2048]{1,0:T(8,128)(2,1)S(1)}, u32[]{:S(2)}, u32[]{:S(2)}) collective-permute-start(bf16[96,2048]{1,0:T(8,128)(2,1)} %collective-permute-done.52.refs_1_), channel_id=1, source_target_pairs={{0,1},{1,0},{2,3},{3,2},{4,5},{5,4},{6,7},{7,6},{8,9},{9,8},{10,11... | collective-permute-start | bytes 1179656 | tf_op jit(solution)/shard_map/ppermute | solution.py:156
  184.4 24.7 %collective-permute-start.58 = (bf16[96,2048]{1,0:T(8,128)(2,1)}, bf16[96,2048]{1,0:T(8,128)(2,1)S(1)}, u32[]{:S(2)}, u32[]{:S(2)}) collective-permute-start(bf16[96,2048]{1,0:T(8,128)(2,1)} %collective-permute-done.53.refs_2_), channel_id=1, source_target_pairs={{0,1},{1,0},{2,3},{3,2},{4,5},{5,4},{6,7},{7,6},{8,9},{9,8},{10,11... | collective-permute-start | bytes 1179656 | tf_op jit(solution)/shard_map/ppermute | solution.py:156
  184.5 26.0 %collective-permute-start.59 = (bf16[48,2048]{1,0:T(8,128)(2,1)}, bf16[48,2048]{1,0:T(8,128)(2,1)}, u32[]{:S(2)}, u32[]{:S(2)}) collective-permute-start(bf16[48,2048]{1,0:T(8,128)(2,1)} %collective-permute-done.54.refs_3_), channel_id=1, source_target_pairs={{0,1},{1,0},{2,3},{3,2},{4,5},{5,4},{6,7},{7,6},{8,9},{9,8},{10,11... | collective-permute-start | bytes 589832 | tf_op jit(solution)/shard_map/ppermute | solution.py:156
  184.9 25.6 %collective-permute-start.60 = (bf16[48,2048]{1,0:T(8,128)(2,1)}, bf16[48,2048]{1,0:T(8,128)(2,1)}, u32[]{:S(2)}, u32[]{:S(2)}) collective-permute-start(bf16[48,2048]{1,0:T(8,128)(2,1)} %collective-permute-done.55.refs_4_), channel_id=1, source_target_pairs={{0,1},{1,0},{2,3},{3,2},{4,5},{5,4},{6,7},{7,6},{8,9},{9,8},{10,11... | collective-permute-start | bytes 589832 | tf_op jit(solution)/shard_map/ppermute | solution.py:156
  208.6 35.3 %collective-permute-start.28 = (bf16[384,2048]{1,0:T(8,128)(2,1)S(1)}, bf16[384,2048]{1,0:T(8,128)(2,1)S(1)}, u32[]{:S(2)}, u32[]{:S(2)}) collective-permute-start(bf16[384,2048]{1,0:T(8,128)(2,1)S(1)} %copy-done.15), channel_id=1, source_target_pairs={{0,1},{1,0},{2,3},{3,2},{4,5},{5,4},{6,7},{7,6},{8,9},{9,8},{10,11... | collective-permute-start | bytes 4718600 | tf_op jit(solution)/shard_map/ppermute | solution.py:156
  210.1 48.7 %collective-permute-start.45 = (bf16[384,2048]{1,0:T(8,128)(2,1)}, bf16[384,2048]{1,0:T(8,128)(2,1)S(1)}, u32[]{:S(2)}, u32[]{:S(2)}) collective-permute-start(bf16[384,2048]{1,0:T(8,128)(2,1)} %get-tuple-element.114), channel_id=1, source_target_pairs={{0,1},{1,0},{2,3},{3,2},{4,5},{5,4},{6,7},{7,6},{8,9},{9,8},{10,11... | collective-permute-start | bytes 4718600 | tf_op jit(solution)/shard_map/ppermute | solution.py:156
  233.8 45.9 %collective-permute-start.62 = (bf16[384,2048]{1,0:T(8,128)(2,1)}, bf16[384,2048]{1,0:T(8,128)(2,1)S(1)}, u32[]{:S(2)}, u32[]{:S(2)}) collective-permute-start(bf16[384,2048]{1,0:T(8,128)(2,1)} %get-tuple-element.116), channel_id=1, source_target_pairs={{0,1},{1,0},{2,3},{3,2},{4,5},{5,4},{6,7},{7,6},{8,9},{9,8},{10,11... | collective-permute-start | bytes 4718600 | tf_op jit(solution)/shard_map/ppermute | solution.py:156
  242.1 64.1 %collective-permute-start.16 = (bf16[96,2048]{1,0:T(8,128)(2,1)S(1)}, bf16[96,2048]{1,0:T(8,128)(2,1)S(1)}, u32[]{:S(2)}, u32[]{:S(2)}) collective-permute-start(bf16[96,2048]{1,0:T(8,128)(2,1)S(1)} %get-tuple-element.124), channel_id=1, source_target_pairs={{0,2},{1,3},{2,0},{3,1},{4,6},{5,7},{6,4},{7,5},{8,10},{9,11},{10,... | collective-permute-start | bytes 1179656 | tf_op jit(solution)/shard_map/ppermute | solution.py:160
  245.0 13.7 %collective-permute-start.31 = (bf16[48,2048]{1,0:T(8,128)(2,1)S(1)}, bf16[48,2048]{1,0:T(8,128)(2,1)S(1)}, u32[]{:S(2)}, u32[]{:S(2)}) collective-permute-start(bf16[48,2048]{1,0:T(8,128)(2,1)S(1)} %get-tuple-element.150), channel_id=1, source_target_pairs={{0,4},{4,0},{8,12},{12,8},{16,20},{20,16},{24,28},{28,24},{1,5},{5... | collective-permute-start | bytes 589832 | tf_op jit(solution)/shard_map/ppermute | solution.py:164
  256.9 49.3 %collective-permute-start.14 = (bf16[96,2048]{1,0:T(8,128)(2,1)S(1)}, bf16[96,2048]{1,0:T(8,128)(2,1)S(1)}, u32[]{:S(2)}, u32[]{:S(2)}) collective-permute-start(bf16[96,2048]{1,0:T(8,128)(2,1)S(1)} %get-tuple-element.123), channel_id=1, source_target_pairs={{0,4},{4,0},{8,12},{12,8},{16,20},{20,16},{24,28},{28,24},{1,5},{5... | collective-permute-start | bytes 1179656 | tf_op jit(solution)/shard_map/ppermute | solution.py:164
  274.5 17.0 %collective-permute-start.49 = (bf16[96,2048]{1,0:T(8,128)(2,1)S(1)}, bf16[96,2048]{1,0:T(8,128)(2,1)S(1)}, u32[]{:S(2)}, u32[]{:S(2)}) collective-permute-start(bf16[96,2048]{1,0:T(8,128)(2,1)S(1)} %get-tuple-element.136), channel_id=1, source_target_pairs={{0,2},{1,3},{2,0},{3,1},{4,6},{5,7},{6,4},{7,5},{8,10},{9,11},{10,... | collective-permute-start | bytes 1179656 | tf_op jit(solution)/shard_map/ppermute | solution.py:160
  288.0 18.3 %collective-permute-start.33 = (bf16[96,2048]{1,0:T(8,128)(2,1)S(1)}, bf16[96,2048]{1,0:T(8,128)(2,1)S(1)}, u32[]{:S(2)}, u32[]{:S(2)}) collective-permute-start(bf16[96,2048]{1,0:T(8,128)(2,1)S(1)} %fusion.11), channel_id=1, source_target_pairs={{0,24},{4,28},{8,0},{12,4},{16,8},{20,12},{24,16},{28,20},{1,25},{... | collective-permute-start | bytes 1179656 | tf_op jit(solution)/shard_map/ppermute | solution.py:168
  299.4 24.0 %collective-permute-start.50 = (bf16[96,2048]{1,0:T(8,128)(2,1)S(1)}, bf16[96,2048]{1,0:T(8,128)(2,1)S(1)}, u32[]{:S(2)}, u32[]{:S(2)}) collective-permute-start(bf16[96,2048]{1,0:T(8,128)(2,1)S(1)} %fusion.9), channel_id=1, source_target_pairs={{0,16},{4,20},{8,24},{12,28},{16,0},{20,4},{24,8},{28,12},{1,17},{... | collective-permute-start | bytes 1179656 | tf_op jit(solution)/shard_map/ppermute | solution.py:168
  304.0 19.4 %collective-permute-start.67 = (bf16[96,2048]{1,0:T(8,128)(2,1)S(1)}, bf16[96,2048]{1,0:T(8,128)(2,1)S(1)}, u32[]{:S(2)}, u32[]{:S(2)}) collective-permute-start(bf16[96,2048]{1,0:T(8,128)(2,1)S(1)} %fusion.7), channel_id=1, source_target_pairs={{0,8},{4,12},{8,16},{12,20},{16,24},{20,28},{24,0},{28,4},{1,9},{5... | collective-permute-start | bytes 1179656 | tf_op jit(solution)/shard_map/ppermute | solution.py:168
  (67 other events, 799.1 us)

commit v2 on v1

--- a/solution.py
+++ b/solution.py
@@ -168,123 +168,133 @@
     return lax.ppermute(a, "ctx", [(i, (i + 2 * steps) % 8) for i in range(8)])
 
 
-def ffn_kernel(*refs, n_parts):
-    parts = refs[:n_parts]
-    gate_ref, first_ref, second_ref, own_ref, other_ref, rows_ref, total_ref = refs[n_parts:]
-    expert, block = pl.program_id(0), pl.program_id(1)
-    first_step = (expert == 0) & (block == 0)
-    last_step = (expert == pl.num_programs(0) - 1) & (block == pl.num_programs(1) - 1)
-
-    @pl.when(first_step)
-    def _():
-        at = 0
-        for part in parts:
-            size = part.shape[0]
-            rows_ref[at : at + size, :] = part[...]
-            at += size
-
-    inner = gelu_tanh(
-        jnp.dot(rows_ref[...], first_ref[0], preferred_element_type=jnp.float32)
-    ) * gate_ref[0]
-    product = jnp.dot(
-        inner.astype(jnp.bfloat16), second_ref[0], preferred_element_type=jnp.float32
-    )
-
-    @pl.when(first_step)
-    def _():
-        total_ref[...] = product
-
-    @pl.when(jnp.logical_not(first_step))
-    def _():
-        total_ref[...] += product
-
-    @pl.when(last_step)
-    def _():
-        half = own_ref.shape[0]
-        own_ref[...] = total_ref[:half].astype(own_ref.dtype)
-        other_ref[...] = total_ref[half:].astype(other_ref.dtype)
-
-
-def dense_ffn(parts, gate, w_in, w_out):
-    rows = sum(p.shape[0] for p in parts)
-    n_exp, width, inner = w_in.shape
-    cut = 512
-    whole = lambda e, f: (0, 0)
-    half = jax.ShapeDtypeStruct((rows // 2, width), jnp.bfloat16)
-    return pl.pallas_call(
-        functools.partial(ffn_kernel, n_parts=len(parts)),
-        grid=(n_exp, inner // cut),
-        in_specs=[pl.BlockSpec(p.shape, whole, pipeline_mode=pl.Buffered(1)) for p in parts]
-        + [
-            pl.BlockSpec((1, rows, 1), lambda e, f: (e, 0, 0)),
-            pl.BlockSpec((1, width, cut), lambda e, f: (e, 0, f)),
-            pl.BlockSpec((1, cut, width), lambda e, f: (e, f, 0)),
-        ],
-        out_specs=[pl.BlockSpec(half.shape, whole)] * 2,
-        out_shape=[half, half],
-        scratch_shapes=[
-            pltpu.VMEM((rows, width), jnp.bfloat16),
-            pltpu.VMEM((rows, width), jnp.float32),
-        ],
-        compiler_params=pltpu.CompilerParams(vmem_limit_bytes=56 << 20),
-        cost_estimate=pl.CostEstimate(
-            flops=4 * n_exp * rows * width * inner,
-            bytes_accessed=4 * n_exp * width * inner + 4 * rows * width,
-            transcendentals=n_exp * rows * inner,
-        ),
-        name="dense_ffn",
-    )(*parts, gate, w_in, w_out)
-
-
-def gather_plane(a):
-    half = a.shape[0] // 2
-    by_y, by_x = swap_y(a), swap_x(a)
-    corner_x, corner_y = swap_x(by_y[:half]), swap_y(by_x[half:])
-    mine = [a, by_y, by_x, corner_x, corner_y]
-    return mine + [swap_core(p) for p in mine]
-
-
-def reduce_plane(own_half, other_half, tok_count):
-    half = tok_count // 2
-    both = own_half.astype(jnp.float32) + swap_core(other_half).astype(jnp.float32)
-    mine, to_y, to_x = (both[i * tok_count : (i + 1) * tok_count] for i in range(3))
-    corner = both[3 * tok_count :].astype(jnp.bfloat16)
-    from_x, from_y = swap_x(corner[:half]), swap_y(corner[half:])
-    to_y = to_y.at[:half].add(from_x.astype(jnp.float32)).astype(jnp.bfloat16)
-    to_x = to_x.at[half:].add(from_y.astype(jnp.float32)).astype(jnp.bfloat16)
-    return mine + swap_y(to_y).astype(jnp.float32) + swap_x(to_x).astype(jnp.float32)
+def gated_ffn(rows, gate, w_in, w_out):
+    n_exp, inner, width = w_out.shape
+    acts = [
+        (
+            gelu_tanh(jnp.dot(rows, w_in[e], preferred_element_type=jnp.float32))
+            * gate[e][:, None]
+        ).astype(jnp.bfloat16)
+        for e in range(n_exp)
+    ]
+    return jnp.dot(
+        jnp.concatenate(acts, axis=1),
+        w_out.reshape(n_exp * inner, width),
+        preferred_element_type=jnp.float32,
+    ).astype(jnp.bfloat16)
+
+
+def after(gate_value, values):
+    return lax.optimization_barrier((gate_value, values))
 
 
 def dense_sum(hidden_f, normed, expert_ids, gate_weights, w_in, w_out):
     tok_count, _ = normed.shape
+    half = tok_count // 2
     n_local = w_in.shape[0]
-    small = jnp.concatenate([expert_ids[0].astype(jnp.float32).T, gate_weights[0].T], axis=0)
-    by_y = swap_y(small)
-    small = jnp.stack([small, by_y])
+    f32, bf16 = jnp.float32, jnp.bfloat16
+    small = jnp.concatenate([expert_ids[0].astype(f32).T, gate_weights[0].T], axis=0)
+    small = jnp.stack([small, swap_y(small)])
     small = jnp.concatenate([small, swap_x(small)])
-    small = jnp.concatenate([small, swap_core(small)])
+    small = jnp.stack([small, swap_core(small)])
     small = [small] + [turn_z(small, k) for k in range(1, 4)]
     local_ids = (
         lax.axis_index("exp") * n_local + jnp.arange(n_local, dtype=jnp.int32)
-    ).astype(jnp.float32)
-
-    gathered, ring = [], normed
-    for k in range(4):
-        if k:
-            ring = turn_z(ring, 1)
-        gathered.append(gather_plane(ring))
+    ).astype(f32)
+
+    def gate_of(slot, core):
+        picked = small[slot][core]
+        ids = jnp.transpose(picked[:, 0:2], (1, 0, 2)).reshape(2, -1)
+        gates = jnp.transpose(picked[:, 2:4], (1, 0, 2)).reshape(2, -1)
+        return jnp.sum(
+            jnp.where(ids[None] == local_ids[:, None, None], gates[None], 0.0), axis=1
+        )
+
+    def neighbours(rows):
+        return [rows, swap_y(rows), swap_x(rows)]
+
+    def corners(near):
+        return [swap_x(near[1][:half]), swap_y(near[2][half:])]
+
+    ring = [normed, turn_z(normed, 1), None, None]
+    near, corner, own, other = [None] * 4, [None] * 4, [None] * 4, [None] * 4
+    near[0] = neighbours(normed)
+    corner[0] = corners(near[0])
+    own[0] = jnp.concatenate(near[0] + corner[0])
+    other[0] = swap_core(own[0])
+    near[1] = neighbours(ring[1])
+    ring[2] = turn_z(ring[1], 1)
+
+    out_own, crossed, parts, flows, planes = [None] * 4, [None] * 4, [None] * 4, [None] * 4, [None] * 4
+
+    def split(slot):
+        both = out_own[slot].astype(f32) + crossed[slot].astype(f32)
+        mine, to_y, to_x = (both[i * tok_count : (i + 1) * tok_count] for i in range(3))
+        last = both[3 * tok_count :].astype(bf16)
+        return mine, to_y, to_x, [swap_x(last[:half]), swap_y(last[half:])]
+
+    def pass_on(slot):
+        mine, to_y, to_x, (from_x, from_y) = parts[slot]
+        to_y = to_y.at[:half].add(from_x.astype(f32)).astype(bf16)
+        to_x = to_x.at[half:].add(from_y.astype(f32)).astype(bf16)
+        return mine, swap_y(to_y), swap_x(to_x)
+
+    def finish(slot):
+        mine, from_y, from_x = flows[slot]
+        plane = mine + from_y.astype(f32) + from_x.astype(f32)
+        return turn_z(plane.astype(bf16), -slot) if slot else plane
+
+    for tick in range(8):
+        slot, core = divmod(tick, 2)
+        rows = other[slot] if core else own[slot]
+        out = gated_ffn(rows, gate_of(slot, core), w_in, w_out)
+        step = tick + 1
+        state = dict(near=near, corner=corner, ring=ring, crossed=crossed, parts=parts, flows=flows)
+        wanted = []
+        if step % 2 and step <= 5:
+            wanted.append(("near", (step + 1) // 2))
+        if step % 2 == 0 and step <= 6:
+            wanted += [("corner", step // 2), ("near", step // 2)]
+            if step <= 4:
+                wanted.append(("ring", (step + 2) // 2))
+        if step % 2 and step >= 3:
+            wanted.append(("crossed", (step - 3) // 2))
+        if step % 2 == 0 and step >= 4:
+            wanted.append(("parts", (step - 4) // 2))
+        if step % 2 and step >= 5:
+            wanted.append(("flows", (step - 5) // 2))
+        out, values = after(out, [state[name][at] for name, at in wanted])
+        for (name, at), value in zip(wanted, values):
+            state[name][at] = value
+        if core:
+            crossed[slot] = swap_core(out)
+        else:
+            out_own[slot] = out
+        if step % 2 and step <= 5:
+            corner[(step + 1) // 2] = corners(near[(step + 1) // 2])
+        if step % 2 == 0 and step <= 6:
+            at = step // 2
+            own[at] = jnp.concatenate(near[at] + corner[at])
+            other[at] = swap_core(own[at])
+            if at < 3:
+                near[at + 1] = neighbours(ring[at + 1])
+                if at < 2:
+                    ring[at + 2] = turn_z(ring[at + 1], 1)
+        if step % 2 and step >= 3:
+            parts[(step - 3) // 2] = split((step - 3) // 2)
+        if step % 2 == 0 and step >= 4:
+            flows[(step - 4) // 2] = pass_on((step - 4) // 2)
+        if step % 2 and step >= 5:
+            planes[(step - 5) // 2] = finish((step - 5) // 2)
+    parts[3] = split(3)
+    planes[1] = finish(1) if planes[1] is None else planes[1]
+    for slot in (2, 3):
+        if flows[slot] is None:
+            flows[slot] = pass_on(slot)
+        planes[slot] = finish(slot)
     total = hidden_f
-    for k in range(4):
-        ids = jnp.transpose(small[k][:, 0:2], (1, 0, 2)).reshape(2, -1)
-        gates = jnp.transpose(small[k][:, 2:4], (1, 0, 2)).reshape(2, -1)
-        gate = jnp.sum(
-            jnp.where(ids[None] == local_ids[:, None, None], gates[None], 0.0), axis=1
-        )
-        own_half, other_half = dense_ffn(gathered[k], gate[..., None], w_in, w_out)
-        plane = reduce_plane(own_half, other_half, tok_count)
-        if k:
-            plane = turn_z(plane.astype(jnp.bfloat16), -k).astype(jnp.float32)
-        total = total + plane
+    for plane in planes:
+        total = total + plane.astype(f32)
     return total
 
 

time: 325 us -> 247 us (0.76); the launches traced: 325 us -> 243 us
  Pallas kernels: 99.6 us -> 6.28 us
  matrix products: 0 us -> 65.4 us
  blocking collectives: 51.3 us -> 0 us
  local copies, waits for them, and re-layouts: 13.2 us -> 6.71 us
    pallas_call x4 -> x0, Pallas kernels: 93.3 us -> none  [dense_ffn(): pl.pallas_call(functools.partial(ffn_kernel, n_parts=len(parts)), grid=(n...]
    dot_general x0 -> x24, matrix products: none -> 65.4 us  [the longest x16 37.1 us: gated_ffn(): jnp.dot(rows, w_in[e], preferred_element_type=jnp.float32)]
    all_to_all x2 -> x0, blocking collectives: 51.3 us -> none  [the longest x1 36.1 us: attention(): lax.all_to_all(outgoing, 'ctx', split_axis=0, concat_axis=0, tiled=True)]
    all_to_all x0 -> x2, starting transfers between devices: none -> 11.2 us  [the longest x1 7.41 us: attention(): lax.all_to_all(outgoing, 'ctx', split_axis=0, concat_axis=0, tiled=True)]
    all_to_all x0 -> x2, waiting for transfers between devices: none -> 10.9 us  [the longest x1 10.9 us: attention(): lax.all_to_all(mixed.reshape(n_ctx, tok_count, piece), 'ctx', split_axis=...]
    ppermute x17, waiting for transfers between devices: 35.6 us -> 27.4 us  [swap_y(): return lax.ppermute(a, 'ctx', [(i, i ^ 1) for i in range(8)])]
    ppermute x17, waiting for transfers between devices: 34.9 us -> 26.7 us  [swap_x(): return lax.ppermute(a, 'exp', [(i, i ^ 2) for i in range(4)])]
    broadcast_in_dim x8, local copies, waits for them, and re-layouts: 5.14 us -> 0.68 us  [gate_of(): jnp.where(ids[None] == local_ids[:, None, None], gates[None], 0.0)]
  transfers between devices with their start and end apart: 68 -> 54, of which waited for: 22 -> 18; matrix products, arithmetic and copies ran while one was open for 4% -> 30% of each run, Pallas kernels for 29% -> 0%
where the time goes in v2:
time: 247 us; the launch traced here: 243 us
  waiting for transfers between devices  92.7 us (38%)
  matrix products  65.4 us (26%)
  starting transfers between devices  63.4 us (26%)
  other arithmetic  7.01 us (3%)
  local copies, waits for them, and re-layouts  6.71 us (3%)
  Pallas kernels  6.28 us (3%)
    dot_general x16, matrix products, gated_ffn(): jnp.dot(rows, w_in[e], preferred_element_type=jnp.float32)  37.1 us
    dot_general x8, matrix products, gated_ffn(): jnp.dot(jnp.concatenate(acts, axis=1), w_out.reshape(n_exp * inner, width...  28.3 us
    ppermute x17, waiting for transfers between devices, swap_y(): return lax.ppermute(a, 'ctx', [(i, i ^ 1) for i in range(8)])  27.4 us
    ppermute x9, waiting for transfers between devices, turn_z(): return lax.ppermute(a, 'ctx', [(i, (i + 2 * steps) % 8) for i in range(8)])  26.7 us
    ppermute x17, waiting for transfers between devices, swap_x(): return lax.ppermute(a, 'exp', [(i, i ^ 2) for i in range(4)])  26.7 us
    ppermute x17, starting transfers between devices, swap_y(): return lax.ppermute(a, 'ctx', [(i, i ^ 1) for i in range(8)])  21.9 us
    ppermute x17, starting transfers between devices, swap_x(): return lax.ppermute(a, 'exp', [(i, i ^ 2) for i in range(4)])  16 us
    ppermute x9, starting transfers between devices, turn_z(): return lax.ppermute(a, 'ctx', [(i, (i + 2 * steps) % 8) for i in range(8)])  12.3 us
  transfers between devices with their start and end apart: 54, of which 18 were waited for; matrix products, arithmetic and copies ran while one was open for 30% of the time, Pallas kernels for 0%

profile of v2, /device:TPU:0, one launch (start us, length us, event | category | flops | bytes accessed | tf_op | source)
XLA Modules:
  0.0 243.0 jit_solution(4038866831752879619)
XLA Ops:
  3.7 7.4 %all-to-all-start = ((bf16[8,96,768]{2,1,0:T(8,128)(2,1)}), bf16[8,96,768]{2,1,0:T(8,128)(2,1)S(1)}, u32[]{:S(2)}, u32[]{:S(2)}) async-start(bf16[8,96,768]{2,1,0:T(8,128)(2,1)} %pad_maximum_fusion), calls=%async_computation | async-start | bytes 2359296 | tf_op jit(solution)/shard_map/all_to_all | solution.py:147
  13.2 5.9 %collective-permute-done.5 = f32[4,96]{1,0:T(4,128)S(1)} collective-permute-done((f32[4,96]{1,0:T(4,128)S(1)}, f32[4,96]{1,0:T(4,128)S(1)}, u32[]{:S(2)}, u32[]{:S(2)}) %collective-permute-start.5) | collective-permute-done | bytes 1568 | tf_op jit(solution)/shard_map/ppermute | solution.py:164
  23.9 3.5 %collective-permute-start.15 = (f32[2,4,4,96]{3,2,1,0:T(4,128)S(1)}, f32[2,4,4,96]{3,2,1,0:T(4,128)S(1)}, u32[]{:S(2)}, u32[]{:S(2)}) collective-permute-start(f32[2,4,4,96]{3,2,1,0:T(4,128)S(1)} %pad_maximum_fusion.1), channel_id=1, source_target_pairs={{0,8},{4,12},{8,16},{12,20},{16,24},{20,28},{24,0},{28,4},{1,9},{5... | collective-permute-start | bytes 36872 | tf_op jit(solution)/shard_map/ppermute | solution.py:168
  31.4 3.5 %collective-permute-done.15 = f32[2,4,4,96]{3,2,1,0:T(4,128)S(1)} collective-permute-done((f32[2,4,4,96]{3,2,1,0:T(4,128)S(1)}, f32[2,4,4,96]{3,2,1,0:T(4,128)S(1)}, u32[]{:S(2)}, u32[]{:S(2)}) %collective-permute-start.15) | collective-permute-done | bytes 12320 | tf_op jit(solution)/shard_map/ppermute | solution.py:168
  35.0 5.9 %collective-permute-done.24 = f32[2,4,4,96]{3,2,1,0:T(4,128)S(1)} collective-permute-done((f32[2,4,4,96]{3,2,1,0:T(4,128)S(1)}, f32[2,4,4,96]{3,2,1,0:T(4,128)S(1)}, u32[]{:S(2)}, u32[]{:S(2)}) %collective-permute-start.24) | collective-permute-done | bytes 12320 | tf_op jit(solution)/shard_map/ppermute | solution.py:168
  42.3 6.3 %attend_heads.1 = bf16[768,256]{1,0:T(8,128)(2,1)} custom-call(bf16[768,768]{1,0:T(8,128)(2,1)} %bitcast.176, bf16[768,768]{1,0:T(8,128)(2,1)} %bitcast.177, bf16[768,768]{1,0:T(8,128)(2,1)} %bitcast.178), custom_call_target="tpu_custom_call" | custom-call | flops 603979776 | bytes 1572864 | tf_op jit(solution)/shard_map/attend_heads/pallas_call | solution.py:119
  48.6 3.8 %all-to-all-start.1 = ((bf16[8,96,256]{2,1,0:T(8,128)(2,1)}), bf16[8,96,256]{2,1,0:T(8,128)(2,1)S(1)}, u32[]{:S(2)}, u32[]{:S(2)}) async-start(bf16[8,96,256]{2,1,0:T(8,128)(2,1)} %bitcast.184), calls=%async_computation.1 | async-start | bytes 786432 | tf_op jit(solution)/shard_map/all_to_all | solution.py:149
  53.4 10.9 %all-to-all-done.1 = bf16[8,96,256]{2,1,0:T(8,128)(2,1)S(1)} async-done(((bf16[8,96,256]{2,1,0:T(8,128)(2,1)}), bf16[8,96,256]{2,1,0:T(8,128)(2,1)S(1)}, u32[]{:S(2)}, u32[]{:S(2)}) %all-to-all-start.1) | async-done | bytes 393248 | tf_op jit(solution)/shard_map/all_to_all | solution.py:149
  67.9 6.8 %collective-permute-done = bf16[96,2048]{1,0:T(8,128)(2,1)S(1)} collective-permute-done((bf16[96,2048]{1,0:T(8,128)(2,1)S(1)}, bf16[96,2048]{1,0:T(8,128)(2,1)S(1)}, u32[]{:S(2)}, u32[]{:S(2)}) %collective-permute-start) | collective-permute-done | bytes 393248 | tf_op jit(solution)/shard_map/ppermute | solution.py:164
  81.5 3.3 %collective-permute-done.3 = bf16[48,2048]{1,0:T(8,128)(2,1)S(1)} collective-permute-done((bf16[48,2048]{1,0:T(8,128)(2,1)S(1)}, bf16[48,2048]{1,0:T(8,128)(2,1)S(1)}, u32[]{:S(2)}, u32[]{:S(2)}) %collective-permute-start.3) | collective-permute-done | bytes 196640 | tf_op jit(solution)/shard_map/ppermute | solution.py:164
  85.0 4.5 %fusion.58 = bf16[384,1024]{1,0:T(8,128)(2,1)S(1)} fusion(bf16[384,2048]{1,0:T(8,128)(2,1)S(1)} %constant_dynamic-update-slice_fusion, f32[384]{0:T(512)S(1)} %get-tuple-element.229, bf16[2,2048,1024]{2,1,0:T(8,128)(2,1)} %param.30), kind=kOutput, calls=%fused_computation.86 | convolution fusion | flops 1614544896 | bytes 6555136 | tf_op jit(solution)/shard_map/dot_general | solution.py:175
  89.5 2.2 fusion.67
  91.7 3.5 %convolution_convert_fusion.6 = bf16[384,2048]{1,0:T(8,128)(2,1)S(1)} fusion(bf16[2048,2048]{1,0:T(8,128)(2,1)S(1)} %bitcast.196, bf16[384,1024]{1,0:T(8,128)(2,1)S(1)} %fusion.67, bf16[384,1024]{1,0:T(8,128)(2,1)S(1)} %fusion.58), kind=kOutput, calls=%fused_computation.42 | convolution fusion | flops 3225157632 | bytes 11534336 | tf_op jit(solution)/shard_map/dot_general | solution.py:180
  99.5 2.2 fusion.49
  101.6 3.5 %convolution_convert_fusion.7 = bf16[384,2048]{1,0:T(8,128)(2,1)S(1)} fusion(bf16[2048,2048]{1,0:T(8,128)(2,1)S(1)} %bitcast.197, bf16[384,1024]{1,0:T(8,128)(2,1)S(1)} %fusion.49, bf16[384,1024]{1,0:T(8,128)(2,1)S(1)} %fusion.40), kind=kOutput, calls=%fused_computation.43 | convolution fusion | flops 3225157632 | bytes 11534336 | tf_op jit(solution)/shard_map/dot_general | solution.py:180
  110.7 2.2 fusion.103
  112.9 3.5 %convolution_convert_fusion.4 = bf16[384,2048]{1,0:T(8,128)(2,1)S(1)} fusion(bf16[2048,2048]{1,0:T(8,128)(2,1)S(1)} %bitcast.198, bf16[384,1024]{1,0:T(8,128)(2,1)S(1)} %fusion.103, bf16[384,1024]{1,0:T(8,128)(2,1)S(1)} %fusion.94), kind=kOutput, calls=%fused_computation.40 | convolution fusion | flops 3225157632 | bytes 11534336 | tf_op jit(solution)/shard_map/dot_general | solution.py:180
  123.0 2.2 fusion.76
  125.2 2.2 fusion.85
  127.3 3.7 %convolution_convert_fusion.5 = bf16[384,2048]{1,0:T(8,128)(2,1)S(1)} fusion(bf16[2048,2048]{1,0:T(8,128)(2,1)S(1)} %bitcast.199, bf16[384,1024]{1,0:T(8,128)(2,1)S(1)} %fusion.85, bf16[384,1024]{1,0:T(8,128)(2,1)S(1)} %fusion.76), kind=kOutput, calls=%fused_computation.41 | convolution fusion | flops 3225157632 | bytes 11534336 | tf_op jit(solution)/shard_map/dot_general | solution.py:180
  134.2 2.2 fusion.112
  139.2 9.8 %collective-permute-done.29 = bf16[96,2048]{1,0:T(8,128)(2,1)S(1)} collective-permute-done((bf16[96,2048]{1,0:T(8,128)(2,1)S(1)}, bf16[96,2048]{1,0:T(8,128)(2,1)S(1)}, u32[]{:S(2)}, u32[]{:S(2)}) %collective-permute-start.29) | collective-permute-done | bytes 393248 | tf_op jit(solution)/shard_map/ppermute | solution.py:160
  150.1 3.5 %convolution_convert_fusion.3 = bf16[384,2048]{1,0:T(8,128)(2,1)S(1)} fusion(bf16[2048,2048]{1,0:T(8,128)(2,1)S(1)} %bitcast.200, bf16[384,1024]{1,0:T(8,128)(2,1)S(1)} %fusion.121, bf16[384,1024]{1,0:T(8,128)(2,1)S(1)} %fusion.112), kind=kOutput, calls=%fused_computation.39 | convolution fusion | flops 3225157632 | bytes 11534336 | tf_op jit(solution)/shard_map/dot_general | solution.py:180
  153.6 3.4 %collective-permute-done.28 = bf16[96,2048]{1,0:T(8,128)(2,1)S(1)} collective-permute-done((bf16[96,2048]{1,0:T(8,128)(2,1)S(1)}, bf16[96,2048]{1,0:T(8,128)(2,1)S(1)}, u32[]{:S(2)}, u32[]{:S(2)}) %collective-permute-start.28) | collective-permute-done | bytes 393248 | tf_op jit(solution)/shard_map/ppermute | solution.py:164
  166.4 3.7 %convolution_convert_fusion.2 = bf16[384,2048]{1,0:T(8,128)(2,1)S(1)} fusion(bf16[2048,2048]{1,0:T(8,128)(2,1)S(1)} %bitcast.201, bf16[384,1024]{1,0:T(8,128)(2,1)S(1)} %fusion.139, bf16[384,1024]{1,0:T(8,128)(2,1)S(1)} %fusion.130), kind=kOutput, calls=%fused_computation.38 | convolution fusion | flops 3225157632 | bytes 11534336 | tf_op jit(solution)/shard_map/dot_general | solution.py:180
  178.7 3.5 %convolution_convert_fusion.1 = bf16[384,2048]{1,0:T(8,128)(2,1)S(1)} fusion(bf16[2048,2048]{1,0:T(8,128)(2,1)S(1)} %bitcast.202, bf16[384,1024]{1,0:T(8,128)(2,1)S(1)} %fusion.157, bf16[384,1024]{1,0:T(8,128)(2,1)S(1)} %fusion.148), kind=kOutput, calls=%fused_computation.37 | convolution fusion | flops 3225157632 | bytes 11534336 | tf_op jit(solution)/shard_map/dot_general | solution.py:180
  186.5 2.4 fusion.175
  188.9 3.5 %convolution_convert_fusion = bf16[384,2048]{1,0:T(8,128)(2,1)S(1)} fusion(bf16[2048,2048]{1,0:T(8,128)(2,1)S(1)} %bitcast.203, bf16[384,1024]{1,0:T(8,128)(2,1)S(1)} %fusion.175, bf16[384,1024]{1,0:T(8,128)(2,1)S(1)} %fusion.166), kind=kOutput, calls=%fused_computation.36 | convolution fusion | flops 3225157632 | bytes 11534336 | tf_op jit(solution)/shard_map/dot_general | solution.py:180
  192.9 4.6 %collective-permute-start.39 = (bf16[96,2048]{1,0:T(8,128)(2,1)S(1)}, bf16[96,2048]{1,0:T(8,128)(2,1)S(1)}, u32[]{:S(2)}, u32[]{:S(2)}) collective-permute-start(bf16[96,2048]{1,0:T(8,128)(2,1)S(1)} %add_convert_fusion.1), channel_id=1, source_target_pairs={{0,24},{4,28},{8,0},{12,4},{16,8},{20,12},{24,16},{28,20},{1,25},{... | collective-permute-start | bytes 1179656 | tf_op jit(solution)/shard_map/ppermute | solution.py:168
  202.9 11.1 %collective-permute-done.47 = bf16[48,2048]{1,0:T(8,128)(2,1)S(1)} collective-permute-done((bf16[48,2048]{1,0:T(8,128)(2,1)S(1)}, bf16[48,2048]{1,0:T(8,128)(2,1)S(1)}, u32[]{:S(2)}, u32[]{:S(2)}) %collective-permute-start.47) | collective-permute-done | bytes 196640 | tf_op jit(solution)/shard_map/ppermute | solution.py:160
  216.3 8.0 %collective-permute-done.48 = bf16[96,2048]{1,0:T(8,128)(2,1)S(1)} collective-permute-done((bf16[96,2048]{1,0:T(8,128)(2,1)S(1)}, bf16[96,2048]{1,0:T(8,128)(2,1)S(1)}, u32[]{:S(2)}, u32[]{:S(2)}) %collective-permute-start.48) | collective-permute-done | bytes 393248 | tf_op jit(solution)/shard_map/ppermute | solution.py:164
  225.3 16.2 %collective-permute-done.45 = bf16[96,2048]{1,0:T(8,128)(2,1)S(1)} collective-permute-done((bf16[96,2048]{1,0:T(8,128)(2,1)S(1)}, bf16[96,2048]{1,0:T(8,128)(2,1)S(1)}, u32[]{:S(2)}, u32[]{:S(2)}) %collective-permute-start.45) | collective-permute-done | bytes 393248 | tf_op jit(solution)/shard_map/ppermute | solution.py:168
  (247 shorter events, 83.0 us)
Async XLA Ops:
  3.7 37.6 %all-to-all-start = ((bf16[8,96,768]{2,1,0:T(8,128)(2,1)}), bf16[8,96,768]{2,1,0:T(8,128)(2,1)S(1)}, u32[]{:S(2)}, u32[]{:S(2)}) async-start(bf16[8,96,768]{2,1,0:T(8,128)(2,1)} %pad_maximum_fusion), calls=%async_computation | async-start | bytes 2359296 | tf_op jit(solution)/shard_map/all_to_all | solution.py:147
  23.9 11.1 %collective-permute-start.15 = (f32[2,4,4,96]{3,2,1,0:T(4,128)S(1)}, f32[2,4,4,96]{3,2,1,0:T(4,128)S(1)}, u32[]{:S(2)}, u32[]{:S(2)}) collective-permute-start(f32[2,4,4,96]{3,2,1,0:T(4,128)S(1)} %pad_maximum_fusion.1), channel_id=1, source_target_pairs={{0,8},{4,12},{8,16},{12,20},{16,24},{20,28},{24,0},{28,4},{1,9},{5... | collective-permute-start | bytes 36872 | tf_op jit(solution)/shard_map/ppermute | solution.py:168
  27.4 13.4 %collective-permute-start.24 = (f32[2,4,4,96]{3,2,1,0:T(4,128)S(1)}, f32[2,4,4,96]{3,2,1,0:T(4,128)S(1)}, u32[]{:S(2)}, u32[]{:S(2)}) collective-permute-start(f32[2,4,4,96]{3,2,1,0:T(4,128)S(1)} %pad_maximum_fusion.1), channel_id=1, source_target_pairs={{0,16},{4,20},{8,24},{12,28},{16,0},{20,4},{24,8},{28,12},{1,17},{... | collective-permute-start | bytes 36872 | tf_op jit(solution)/shard_map/ppermute | solution.py:168
  29.5 11.8 %collective-permute-start.35 = (f32[2,4,4,96]{3,2,1,0:T(4,128)S(1)}, f32[2,4,4,96]{3,2,1,0:T(4,128)S(1)}, u32[]{:S(2)}, u32[]{:S(2)}) collective-permute-start(f32[2,4,4,96]{3,2,1,0:T(4,128)S(1)} %pad_maximum_fusion.1), channel_id=1, source_target_pairs={{0,24},{4,28},{8,0},{12,4},{16,8},{20,12},{24,16},{28,20},{1,25},{... | collective-permute-start | bytes 36872 | tf_op jit(solution)/shard_map/ppermute | solution.py:168
  48.6 15.7 %all-to-all-start.1 = ((bf16[8,96,256]{2,1,0:T(8,128)(2,1)}), bf16[8,96,256]{2,1,0:T(8,128)(2,1)S(1)}, u32[]{:S(2)}, u32[]{:S(2)}) async-start(bf16[8,96,256]{2,1,0:T(8,128)(2,1)} %bitcast.184), calls=%async_computation.1 | async-start | bytes 786432 | tf_op jit(solution)/shard_map/all_to_all | solution.py:149
  66.3 10.7 %collective-permute-start.1 = (bf16[96,2048]{1,0:T(8,128)(2,1)S(1)}, bf16[96,2048]{1,0:T(8,128)(2,1)S(1)}, u32[]{:S(2)}, u32[]{:S(2)}) collective-permute-start(bf16[96,2048]{1,0:T(8,128)(2,1)S(1)} %get-tuple-element.242), channel_id=1, source_target_pairs={{0,2},{1,3},{2,0},{3,1},{4,6},{5,7},{6,4},{7,5},{8,10},{9,11},{10,... | collective-permute-start | bytes 1179656 | tf_op jit(solution)/shard_map/ppermute | solution.py:160
  67.8 11.3 %collective-permute-start.8 = (bf16[96,2048]{1,0:T(8,128)(2,1)S(1)}, bf16[96,2048]{1,0:T(8,128)(2,1)S(1)}, u32[]{:S(2)}, u32[]{:S(2)}) collective-permute-start(bf16[96,2048]{1,0:T(8,128)(2,1)S(1)} %get-tuple-element.242), channel_id=1, source_target_pairs={{0,8},{4,12},{8,16},{12,20},{16,24},{20,28},{24,0},{28,4},{1,9},{5... | collective-permute-start | bytes 1179656 | tf_op jit(solution)/shard_map/ppermute | solution.py:168
  79.1 16.1 %collective-permute-start.10 = (bf16[96,2048]{1,0:T(8,128)(2,1)S(1)}, bf16[96,2048]{1,0:T(8,128)(2,1)S(1)}, u32[]{:S(2)}, u32[]{:S(2)}) collective-permute-start(bf16[96,2048]{1,0:T(8,128)(2,1)S(1)} %collective-permute-done.8), channel_id=1, source_target_pairs={{0,2},{1,3},{2,0},{3,1},{4,6},{5,7},{6,4},{7,5},{8,10},{9,11},{10,... | collective-permute-start | bytes 1179656 | tf_op jit(solution)/shard_map/ppermute | solution.py:160
  79.7 15.5 %collective-permute-start.9 = (bf16[96,2048]{1,0:T(8,128)(2,1)S(1)}, bf16[96,2048]{1,0:T(8,128)(2,1)S(1)}, u32[]{:S(2)}, u32[]{:S(2)}) collective-permute-start(bf16[96,2048]{1,0:T(8,128)(2,1)S(1)} %collective-permute-done.8), channel_id=1, source_target_pairs={{0,4},{4,0},{8,12},{12,8},{16,20},{20,16},{24,28},{28,24},{1,5},{5... | collective-permute-start | bytes 1179656 | tf_op jit(solution)/shard_map/ppermute | solution.py:164
  80.6 24.5 %collective-permute-start.13 = (bf16[96,2048]{1,0:T(8,128)(2,1)S(1)}, bf16[96,2048]{1,0:T(8,128)(2,1)S(1)}, u32[]{:S(2)}, u32[]{:S(2)}) collective-permute-start(bf16[96,2048]{1,0:T(8,128)(2,1)S(1)} %collective-permute-done.8), channel_id=1, source_target_pairs={{0,8},{4,12},{8,16},{12,20},{16,24},{20,28},{24,0},{28,4},{1,9},{5... | collective-permute-start | bytes 1179656 | tf_op jit(solution)/shard_map/ppermute | solution.py:168
  84.9 12.4 %collective-permute-start.4 = (bf16[384,2048]{1,0:T(8,128)(2,1)S(1)}, bf16[384,2048]{1,0:T(8,128)(2,1)S(1)}, u32[]{:S(2)}, u32[]{:S(2)}) collective-permute-start(bf16[384,2048]{1,0:T(8,128)(2,1)S(1)} %constant_dynamic-update-slice_fusion), channel_id=1, source_target_pairs={{0,1},{1,0},{2,3},{3,2},{4,5},{5,4},{6,7},{7,6},{8,9},{9,8},{10,11... | collective-permute-start | bytes 4718600 | tf_op jit(solution)/shard_map/ppermute | solution.py:156
  105.1 11.3 %collective-permute-start.16 = (bf16[96,2048]{1,0:T(8,128)(2,1)S(1)}, bf16[96,2048]{1,0:T(8,128)(2,1)S(1)}, u32[]{:S(2)}, u32[]{:S(2)}) collective-permute-start(bf16[96,2048]{1,0:T(8,128)(2,1)S(1)} %collective-permute-done.13), channel_id=1, source_target_pairs={{0,4},{4,0},{8,12},{12,8},{16,20},{20,16},{24,28},{28,24},{1,5},{5... | collective-permute-start | bytes 1179656 | tf_op jit(solution)/shard_map/ppermute | solution.py:164
  107.8 23.4 %collective-permute-start.21 = (bf16[96,2048]{1,0:T(8,128)(2,1)S(1)}, bf16[96,2048]{1,0:T(8,128)(2,1)S(1)}, u32[]{:S(2)}, u32[]{:S(2)}) collective-permute-start(bf16[96,2048]{1,0:T(8,128)(2,1)S(1)} %collective-permute-done.13), channel_id=1, source_target_pairs={{0,8},{4,12},{8,16},{12,20},{16,24},{20,28},{24,0},{28,4},{1,9},{5... | collective-permute-start | bytes 1179656 | tf_op jit(solution)/shard_map/ppermute | solution.py:168
  108.0 13.2 %collective-permute-start.14 = (bf16[384,2048]{1,0:T(8,128)(2,1)S(1)}, bf16[384,2048]{1,0:T(8,128)(2,1)S(1)}, u32[]{:S(2)}, u32[]{:S(2)}) collective-permute-start(bf16[384,2048]{1,0:T(8,128)(2,1)S(1)} %constant_dynamic-update-slice_fusion.5), channel_id=1, source_target_pairs={{0,1},{1,0},{2,3},{3,2},{4,5},{5,4},{6,7},{7,6},{8,9},{9,8},{10,11... | collective-permute-start | bytes 4718600 | tf_op jit(solution)/shard_map/ppermute | solution.py:156
  118.7 12.6 %collective-permute-start.22 = (bf16[48,2048]{1,0:T(8,128)(2,1)S(1)}, bf16[48,2048]{1,0:T(8,128)(2,1)S(1)}, u32[]{:S(2)}, u32[]{:S(2)}) collective-permute-start(bf16[48,2048]{1,0:T(8,128)(2,1)S(1)} %get-tuple-element.273), channel_id=1, source_target_pairs={{0,2},{1,3},{2,0},{3,1},{4,6},{5,7},{6,4},{7,5},{8,10},{9,11},{10,... | collective-permute-start | bytes 589832 | tf_op jit(solution)/shard_map/ppermute | solution.py:160
  119.3 12.0 %collective-permute-start.23 = (bf16[48,2048]{1,0:T(8,128)(2,1)S(1)}, bf16[48,2048]{1,0:T(8,128)(2,1)S(1)}, u32[]{:S(2)}, u32[]{:S(2)}) collective-permute-start(bf16[48,2048]{1,0:T(8,128)(2,1)S(1)} %get-tuple-element.272), channel_id=1, source_target_pairs={{0,4},{4,0},{8,12},{12,8},{16,20},{20,16},{24,28},{28,24},{1,5},{5... | collective-permute-start | bytes 589832 | tf_op jit(solution)/shard_map/ppermute | solution.py:164
  120.4 10.9 %collective-permute-start.19 = (bf16[48,2048]{1,0:T(8,128)(2,1)S(1)}, bf16[48,2048]{1,0:T(8,128)(2,1)S(1)}, u32[]{:S(2)}, u32[]{:S(2)}) collective-permute-start(bf16[48,2048]{1,0:T(8,128)(2,1)S(1)} %slice.412), channel_id=1, source_target_pairs={{0,2},{1,3},{2,0},{3,1},{4,6},{5,7},{6,4},{7,5},{8,10},{9,11},{10,... | collective-permute-start | bytes 589832 | tf_op jit(solution)/shard_map/ppermute | solution.py:160
  131.3 25.7 %collective-permute-start.25 = (bf16[96,2048]{1,0:T(8,128)(2,1)S(1)}, bf16[96,2048]{1,0:T(8,128)(2,1)S(1)}, u32[]{:S(2)}, u32[]{:S(2)}) collective-permute-start(bf16[96,2048]{1,0:T(8,128)(2,1)S(1)} %collective-permute-done.21), channel_id=1, source_target_pairs={{0,4},{4,0},{8,12},{12,8},{16,20},{20,16},{24,28},{28,24},{1,5},{5... | collective-permute-start | bytes 1179656 | tf_op jit(solution)/shard_map/ppermute | solution.py:164
  131.7 25.3 %collective-permute-start.26 = (bf16[96,2048]{1,0:T(8,128)(2,1)S(1)}, bf16[96,2048]{1,0:T(8,128)(2,1)S(1)}, u32[]{:S(2)}, u32[]{:S(2)}) collective-permute-start(bf16[96,2048]{1,0:T(8,128)(2,1)S(1)} %collective-permute-done.21), channel_id=1, source_target_pairs={{0,2},{1,3},{2,0},{3,1},{4,6},{5,7},{6,4},{7,5},{8,10},{9,11},{10,... | collective-permute-start | bytes 1179656 | tf_op jit(solution)/shard_map/ppermute | solution.py:160
  133.1 15.9 %collective-permute-start.29 = (bf16[96,2048]{1,0:T(8,128)(2,1)S(1)}, bf16[96,2048]{1,0:T(8,128)(2,1)S(1)}, u32[]{:S(2)}, u32[]{:S(2)}) collective-permute-start(bf16[96,2048]{1,0:T(8,128)(2,1)S(1)} %convert_element_type.261), channel_id=1, source_target_pairs={{0,2},{1,3},{2,0},{3,1},{4,6},{5,7},{6,4},{7,5},{8,10},{9,11},{10,... | collective-permute-start | bytes 1179656 | tf_op jit(solution)/shard_map/ppermute | solution.py:160
  134.1 28.0 %collective-permute-start.30 = (bf16[384,2048]{1,0:T(8,128)(2,1)S(1)}, bf16[384,2048]{1,0:T(8,128)(2,1)S(1)}, u32[]{:S(2)}, u32[]{:S(2)}) collective-permute-start(bf16[384,2048]{1,0:T(8,128)(2,1)S(1)} %constant_dynamic-update-slice_fusion.10), channel_id=1, source_target_pairs={{0,1},{1,0},{2,3},{3,2},{4,5},{5,4},{6,7},{7,6},{8,9},{9,8},{10,11... | collective-permute-start | bytes 4718600 | tf_op jit(solution)/shard_map/ppermute | solution.py:156
  136.3 20.7 %collective-permute-start.27 = (bf16[384,2048]{1,0:T(8,128)(2,1)S(1)}, bf16[384,2048]{1,0:T(8,128)(2,1)S(1)}, u32[]{:S(2)}, u32[]{:S(2)}) collective-permute-start(bf16[384,2048]{1,0:T(8,128)(2,1)S(1)} %convolution_convert_fusion.5), channel_id=1, source_target_pairs={{0,1},{1,0},{2,3},{3,2},{4,5},{5,4},{6,7},{7,6},{8,9},{9,8},{10,11... | collective-permute-start | bytes 4718600 | tf_op jit(solution)/shard_map/ppermute | solution.py:156
  157.8 12.6 %collective-permute-start.33 = (bf16[48,2048]{1,0:T(8,128)(2,1)S(1)}, bf16[48,2048]{1,0:T(8,128)(2,1)S(1)}, u32[]{:S(2)}, u32[]{:S(2)}) collective-permute-start(bf16[48,2048]{1,0:T(8,128)(2,1)S(1)} %get-tuple-element.271), channel_id=1, source_target_pairs={{0,2},{1,3},{2,0},{3,1},{4,6},{5,7},{6,4},{7,5},{8,10},{9,11},{10,... | collective-permute-start | bytes 589832 | tf_op jit(solution)/shard_map/ppermute | solution.py:160
  158.8 11.6 %collective-permute-start.34 = (bf16[48,2048]{1,0:T(8,128)(2,1)S(1)}, bf16[48,2048]{1,0:T(8,128)(2,1)S(1)}, u32[]{:S(2)}, u32[]{:S(2)}) collective-permute-start(bf16[48,2048]{1,0:T(8,128)(2,1)S(1)} %get-tuple-element.270), channel_id=1, source_target_pairs={{0,4},{4,0},{8,12},{12,8},{16,20},{20,16},{24,28},{28,24},{1,5},{5... | collective-permute-start | bytes 589832 | tf_op jit(solution)/shard_map/ppermute | solution.py:164
  170.5 11.7 %collective-permute-start.38 = (bf16[96,2048]{1,0:T(8,128)(2,1)S(1)}, bf16[96,2048]{1,0:T(8,128)(2,1)S(1)}, u32[]{:S(2)}, u32[]{:S(2)}) collective-permute-start(bf16[96,2048]{1,0:T(8,128)(2,1)S(1)} %convert_element_type.275), channel_id=1, source_target_pairs={{0,2},{1,3},{2,0},{3,1},{4,6},{5,7},{6,4},{7,5},{8,10},{9,11},{10,... | collective-permute-start | bytes 1179656 | tf_op jit(solution)/shard_map/ppermute | solution.py:160
  192.9 32.4 %collective-permute-start.39 = (bf16[96,2048]{1,0:T(8,128)(2,1)S(1)}, bf16[96,2048]{1,0:T(8,128)(2,1)S(1)}, u32[]{:S(2)}, u32[]{:S(2)}) collective-permute-start(bf16[96,2048]{1,0:T(8,128)(2,1)S(1)} %add_convert_fusion.1), channel_id=1, source_target_pairs={{0,24},{4,28},{8,0},{12,4},{16,8},{20,12},{24,16},{28,20},{1,25},{... | collective-permute-start | bytes 1179656 | tf_op jit(solution)/shard_map/ppermute | solution.py:168
  197.6 18.4 %collective-permute-start.43 = (bf16[96,2048]{1,0:T(8,128)(2,1)S(1)}, bf16[96,2048]{1,0:T(8,128)(2,1)S(1)}, u32[]{:S(2)}, u32[]{:S(2)}) collective-permute-start(bf16[96,2048]{1,0:T(8,128)(2,1)S(1)} %convert_element_type.286), channel_id=1, source_target_pairs={{0,4},{4,0},{8,12},{12,8},{16,20},{20,16},{24,28},{28,24},{1,5},{5... | collective-permute-start | bytes 1179656 | tf_op jit(solution)/shard_map/ppermute | solution.py:164
  198.8 17.3 %collective-permute-start.44 = (bf16[96,2048]{1,0:T(8,128)(2,1)S(1)}, bf16[96,2048]{1,0:T(8,128)(2,1)S(1)}, u32[]{:S(2)}, u32[]{:S(2)}) collective-permute-start(bf16[96,2048]{1,0:T(8,128)(2,1)S(1)} %convert_element_type.289), channel_id=1, source_target_pairs={{0,2},{1,3},{2,0},{3,1},{4,6},{5,7},{6,4},{7,5},{8,10},{9,11},{10,... | collective-permute-start | bytes 1179656 | tf_op jit(solution)/shard_map/ppermute | solution.py:160
  201.1 12.9 %collective-permute-start.47 = (bf16[48,2048]{1,0:T(8,128)(2,1)S(1)}, bf16[48,2048]{1,0:T(8,128)(2,1)S(1)}, u32[]{:S(2)}, u32[]{:S(2)}) collective-permute-start(bf16[48,2048]{1,0:T(8,128)(2,1)S(1)} %get-tuple-element.266), channel_id=1, source_target_pairs={{0,2},{1,3},{2,0},{3,1},{4,6},{5,7},{6,4},{7,5},{8,10},{9,11},{10,... | collective-permute-start | bytes 589832 | tf_op jit(solution)/shard_map/ppermute | solution.py:160
  201.7 12.3 %collective-permute-start.49 = (bf16[48,2048]{1,0:T(8,128)(2,1)S(1)}, bf16[48,2048]{1,0:T(8,128)(2,1)S(1)}, u32[]{:S(2)}, u32[]{:S(2)}) collective-permute-start(bf16[48,2048]{1,0:T(8,128)(2,1)S(1)} %get-tuple-element.267), channel_id=1, source_target_pairs={{0,4},{4,0},{8,12},{12,8},{16,20},{20,16},{24,28},{28,24},{1,5},{5... | collective-permute-start | bytes 589832 | tf_op jit(solution)/shard_map/ppermute | solution.py:164
  216.2 25.3 %collective-permute-start.45 = (bf16[96,2048]{1,0:T(8,128)(2,1)S(1)}, bf16[96,2048]{1,0:T(8,128)(2,1)S(1)}, u32[]{:S(2)}, u32[]{:S(2)}) collective-permute-start(bf16[96,2048]{1,0:T(8,128)(2,1)S(1)} %add_convert_fusion), channel_id=1, source_target_pairs={{0,16},{4,20},{8,24},{12,28},{16,0},{20,4},{24,8},{28,12},{1,17},{... | collective-permute-start | bytes 1179656 | tf_op jit(solution)/shard_map/ppermute | solution.py:168
  225.2 16.3 %collective-permute-start.51 = (bf16[96,2048]{1,0:T(8,128)(2,1)S(1)}, bf16[96,2048]{1,0:T(8,128)(2,1)S(1)}, u32[]{:S(2)}, u32[]{:S(2)}) collective-permute-start(bf16[96,2048]{1,0:T(8,128)(2,1)S(1)} %fusion.239), channel_id=1, source_target_pairs={{0,8},{4,12},{8,16},{12,20},{16,24},{20,28},{24,0},{28,4},{1,9},{5... | collective-permute-start | bytes 1179656 | tf_op jit(solution)/shard_map/ppermute | solution.py:168
  (33 other events, 283.7 us)
